TPU v7x, 32 devices: a whole 2x2x4 slice. The times are simulated.
32 devices in a mesh: groups: 2 (over x), gx: 16 (over z, y, core), gy: 1.
Axes of the slice: x: 2, y: 2, z: 4, core: 2. Of those that a mesh axis runs over, the one named last changes fastest.
Arguments:
- field: float32 [64, 32, 2048], P(('groups', 'gx'), 'gy'), parts along dimension 0, may hold values from -6 to 6
- spectral: float32 [32, 32, 16, 2, 32, 32], P('gy', 'gx'), may hold values from -2.1213202 to 2.1213202
- conv_first: float32 [3, 3, 3, 32, 32], replicated, may hold values from -0.21875 to 0.21875
- conv_second: float32 [3, 3, 3, 32, 32], replicated, may hold values from -0.21875 to 0.21875
- bias: float32 [32], replicated, may hold values from -3 to 3
Outputs:
- block_output: float32 [64, 32, 2048], P(('groups', 'gx'), 'gy'), parts along dimension 0
There are 2 independent parts, one for each index of `groups`. A program takes and returns all parts, laid end to end along the dimension named above; an argument that names none is the same for every part. Nothing has to cross between parts.
All inputs are finite; a program needn't handle non-finite values.
Results may differ from a plain program's by a relative error of at most 0.000057.
Values sent between devices are 32-bit elements; how exact they have to be, the bound alone decides.
A program may use at most 128 MiB of HBM per device.

v0:
```python
import math

import jax
import jax.numpy as jnp
from jax import lax
from jax.sharding import PartitionSpec as P

CH = 32
NZ = 64
MX = 32
MY = 32
MZ = 16


HIGHEST = lax.Precision.HIGHEST


def with_halo(cells, sides, width):
    for axis, dim in sides:
        count = lax.axis_size(axis)
        ends = count - 1
        head = lax.slice_in_dim(cells, 0, width, axis=dim)
        tail = lax.slice_in_dim(cells, cells.shape[dim] - width, cells.shape[dim], axis=dim)
        cells = jnp.concatenate(
            [
                lax.ppermute(tail, axis, [(i, (i + 1) % count) for i in range(ends)]),
                cells,
                lax.ppermute(head, axis, [((i + 1) % count, i) for i in range(ends)]),
            ],
            axis=dim,
        )
    return cells


def frequency(position, length, retained):
    return jnp.where(position < retained // 2, position, length - retained + position)


def angle_table(first_list, second_list, length):
    product = first_list[:, None] * second_list[None, :] % length
    angles = product.astype(jnp.float32) * (2.0 * math.pi / length)
    return (jnp.cos(angles), jnp.sin(angles))


def rotate_sum(cos_table, sin_table, values, pattern, direction_sign):
    real_part = values[:, :, 0]
    imag_part = values[:, :, 1]
    out_real = jnp.einsum(
        pattern, cos_table, real_part, precision=HIGHEST
    ) + direction_sign * jnp.einsum(pattern, sin_table, imag_part, precision=HIGHEST)
    out_imag = jnp.einsum(
        pattern, cos_table, imag_part, precision=HIGHEST
    ) - direction_sign * jnp.einsum(pattern, sin_table, real_part, precision=HIGHEST)
    return jnp.stack([out_real, out_imag], axis=2)


def convolve(padded, weight):
    extent_x = padded.shape[0] - 2
    extent_y = padded.shape[1] - 2
    volume = padded.reshape(padded.shape[0], padded.shape[1], NZ, CH)
    volume = jnp.pad(volume, ((0, 0), (0, 0), (1, 1), (0, 0)))
    kernel = weight.reshape(3, 3, 3 * CH, CH)

    def plane(start):
        slab = lax.dynamic_slice_in_dim(volume, start, 3, 0)
        accumulated = jnp.zeros((extent_y, NZ, CH), jnp.float32)
        for shift_x in range(3):
            for shift_y in range(3):
                windowed = slab[shift_x, shift_y : shift_y + extent_y]
                stacked = jnp.concatenate(
                    [windowed[:, shift_z : shift_z + NZ] for shift_z in range(3)], axis=2
                )
                accumulated = accumulated + jnp.einsum(
                    "yzi,io->yzo", stacked, kernel[shift_x, shift_y], precision=HIGHEST
                )
        return accumulated

    return lax.map(plane, jnp.arange(extent_x, dtype=jnp.int32))


def mode_mix(inputs, matrix):
    return jnp.einsum("bazi,bazio->bazo", inputs, matrix, precision=HIGHEST)


def body(field, spectral, conv_first, conv_second, bias):
    cells_x, cells_y, merged_width = field.shape
    devices_x = lax.axis_size("gx")
    devices_y = lax.axis_size("gy")
    extent_x = cells_x * devices_x
    extent_y = cells_y * devices_y
    owned_x = MX // devices_x
    owned_y = MY // devices_y
    y_places = lax.axis_index("gy") * cells_y + jnp.arange(cells_y, dtype=jnp.int32)
    mode_width = MZ * CH
    volume = field.reshape(cells_x, cells_y, NZ, CH)
    z_modes_index = jnp.arange(MZ, dtype=jnp.int32)
    z_cos, z_sin = angle_table(z_modes_index, jnp.arange(NZ, dtype=jnp.int32), NZ)
    z_real = jnp.einsum("xyzc,kz->xykc", volume, z_cos, precision=HIGHEST)
    z_imag = -jnp.einsum("xyzc,kz->xykc", volume, z_sin, precision=HIGHEST)
    z_spectrum = jnp.stack([z_real, z_imag], axis=2).reshape(cells_x, cells_y, 2, mode_width)
    cos_table, sin_table = angle_table(
        frequency(jnp.arange(MX, dtype=jnp.int32), extent_x, MX),
        jnp.arange(extent_x, dtype=jnp.int32),
        extent_x,
    )
    kept_modes = rotate_sum(
        cos_table,
        sin_table,
        lax.all_to_all(z_spectrum, "gx", split_axis=1, concat_axis=0, tiled=True),
        "kx,xym->kym",
        1.0,
    )
    x_modes = lax.all_to_all(kept_modes, "gx", split_axis=0, concat_axis=1, tiled=True)
    row_index = jnp.arange(owned_y * lax.axis_size("gy"), dtype=jnp.int32)
    cos_table, sin_table = angle_table(frequency(row_index, extent_y, MY), y_places, extent_y)
    all_modes = lax.psum_scatter(
        rotate_sum(cos_table, sin_table, x_modes, "ky,xym->kxm", 1.0),
        "gy",
        scatter_dimension=0,
        tiled=True,
    )
    complex_parts = all_modes.reshape(owned_y, owned_x, 2, MZ, CH)
    real_inputs = complex_parts[:, :, 0]
    imag_inputs = complex_parts[:, :, 1]
    weight_real = spectral[:, :, :, 0]
    weight_imag = spectral[:, :, :, 1]
    mixed_real = mode_mix(real_inputs, weight_real) - mode_mix(imag_inputs, weight_imag)
    mixed_imag = mode_mix(real_inputs, weight_imag) + mode_mix(imag_inputs, weight_real)
    mixed = jnp.stack([mixed_real, mixed_imag], axis=2).reshape(owned_y, owned_x, 2, mode_width)
    portion = lax.all_gather(mixed, "gy", axis=0, tiled=True)
    row_index = jnp.arange(portion.shape[0], dtype=jnp.int32)
    cos_table, sin_table = angle_table(y_places, frequency(row_index, extent_y, MY), extent_y)
    y_cells = rotate_sum(cos_table, sin_table, portion, "yk,kxm->xym", -1.0)
    cos_table, sin_table = angle_table(
        jnp.arange(extent_x, dtype=jnp.int32),
        frequency(jnp.arange(MX, dtype=jnp.int32), extent_x, MX),
        extent_x,
    )
    cell_lines = rotate_sum(
        cos_table,
        sin_table,
        lax.all_to_all(y_cells, "gx", split_axis=1, concat_axis=0, tiled=True),
        "xk,kym->xym",
        -1.0,
    )
    planes = lax.all_to_all(cell_lines, "gx", split_axis=0, concat_axis=1, tiled=True)
    z_weights = jnp.where(z_modes_index == 0, 1.0, 2.0).astype(jnp.float32) / (
        extent_x * extent_y * NZ
    )
    planes_split = planes.reshape(cells_x, cells_y, 2, MZ, CH)
    spectral_part = jnp.einsum(
        "xykc,kz->xyzc", planes_split[:, :, 0], z_cos * z_weights[:, None], precision=HIGHEST
    ) - jnp.einsum(
        "xykc,kz->xyzc", planes_split[:, :, 1], z_sin * z_weights[:, None], precision=HIGHEST
    )
    with_rim = with_halo(field, (("gx", 0), ("gy", 1)), 1)
    first_hidden = jax.nn.gelu(convolve(with_rim, conv_first), approximate=False).reshape(
        cells_x, cells_y, merged_width
    )
    hidden_block = with_halo(first_hidden, (("gx", 0), ("gy", 1)), 1)
    second_branch = convolve(hidden_block, conv_second)
    result = jax.nn.gelu(spectral_part + second_branch + bias, approximate=False)
    return result.reshape(cells_x, cells_y, merged_width)


def solution(mesh):
    in_specs = (
        P(("groups", "gx"), "gy", None),
        P("gy", "gx", None, None, None, None),
        P(),
        P(),
        P(),
    )
    out_specs = P(("groups", "gx"), "gy", None)
    return jax.shard_map(body, mesh=mesh, in_specs=in_specs, out_specs=out_specs, check_vma=False)
```

profile of v0, /device:TPU:0, one launch (start us, length us, event | category | flops | bytes accessed | tf_op | source)
XLA Modules:
  0.0 328.5 jit_solution(4292039270730394222)
XLA Ops:
  14.2 9.4 %all-to-all-start = ((f32[2,32,2,512]{3,0,2,1:T(2,128)}), f32[2,32,2,512]{3,0,2,1:T(2,128)}, u32[]{:S(2)}, u32[]{:S(2)}) async-start(f32[2,32,2,512]{3,0,2,1:T(2,128)} %pad_maximum_fusion.2), calls=%async_computation | async-start | bytes 524288 | tf_op jit(solution)/shard_map/all_to_all | solution.py:109
  27.7 5.3 %pad.7 = f32[4,34,66,32]{3,2,0,1:T(8,128)} pad(f32[4,34,64,32]{3,2,0,1:T(8,128)} %reshape.57, f32[]{:T(128)} %constant.66.clone.1), padding=0_0x0_0x1_1x0_0 | pad | bytes 2263044 | tf_op jit(solution)/shard_map/jit(_pad)/pad | solution.py:61
  33.1 78.4 %while.20 = (s32[]{:T(128)}, f32[2,32,64,32]{2,3,1,0:T(8,128)S(1)}, s32[2]{0:T(128)S(1)}, f32[4,34,66,32]{3,2,0,1:T(8,128)}, f32[3,3,96,32]{2,3,1,0:T(8,128)S(1)...) while((s32[]{:T(128)}, f32[2,32,64,32]{2,3,1,0:T(8,128)S(1)}, s32[2]{0:T(128)S(1)}, ...), condition=%wide.region_1.2_spmd, body=%wide.region_0.1_spmd.sunk | while | flops 683540480 | bytes 54296804 | solution.py:78
  35.8 5.2 %dynamic-slice_bitcast_fusion.20 = (f32[32,66,32]{2,1,0:T(8,128)S(1)}, f32[32,66,32]{2,1,0:T(8,128)S(1)}, f32[32,66,32]{2,1,0:T(8,128)S(1)}, f32[32,66,32]{2,1,0...) fusion(f32[4,34,66,32]{3,2,0,1:T(8,128)} %get-tuple-element.434, ...), kind=kLoop, calls=%fused_computation.10.clone.1 | loop fusion | bytes 4866068 | tf_op jit(solution)/shard_map/while/body/eval_jaxpr/squeeze | solution.py:69
  45.2 3.1 convolution_add_fusion.34
  52.1 3.1 convolution_add_fusion.36
  59.0 3.1 convolution_add_fusion.38
  65.9 3.1 convolution_add_fusion.40
  74.6 5.4 %dynamic-slice_bitcast_fusion.20 = (f32[32,66,32]{2,1,0:T(8,128)S(1)}, f32[32,66,32]{2,1,0:T(8,128)S(1)}, f32[32,66,32]{2,1,0:T(8,128)S(1)}, f32[32,66,32]{2,1,0...) fusion(f32[4,34,66,32]{3,2,0,1:T(8,128)} %get-tuple-element.434, ...), kind=kLoop, calls=%fused_computation.10.clone.1 | loop fusion | bytes 4866068 | tf_op jit(solution)/shard_map/while/body/eval_jaxpr/squeeze | solution.py:69
  84.2 3.1 convolution_add_fusion.34
  91.1 3.1 convolution_add_fusion.36
  98.0 3.1 convolution_add_fusion.38
  104.9 3.1 convolution_add_fusion.40
  128.7 7.4 %all-to-all-start.1 = ((f32[32,2,2,512]{3,1,2,0:T(2,128)}), f32[32,2,2,512]{3,1,2,0:T(2,128)S(1)}, u32[]{:S(2)}, u32[]{:S(2)}) async-start(f32[32,2,2,512]{3,1,2,0:T(2,128)} %copy.35), calls=%async_computation.1 | async-start | bytes 524288 | tf_op jit(solution)/shard_map/all_to_all | solution.py:113
  137.2 8.9 %all-to-all-done.1 = f32[32,2,2,512]{3,1,2,0:T(2,128)S(1)} async-done(((f32[32,2,2,512]{3,1,2,0:T(2,128)}), f32[32,2,2,512]{3,1,2,0:T(2,128)S(1)}, u32[]{:S(2)}, u32[]{:S(2)}) %all-to-all-start.1) | async-done | bytes 262176 | tf_op jit(solution)/shard_map/all_to_all | solution.py:113
  147.6 15.9 %fusion.152 = f32[32,2,16,1,32]{4,3,2,1,0:T(1,128)S(1)} fusion(f32[32,2,16,2,32,32]{5,4,3,2,1,0:T(8,128)} %param.10, f32[32,2,16,32,1]{3,2,0,1,4:T(8,128)S(1)} %reshape.87), kind=kOutput, calls=%fused_computation.186 | convolution fusion | flops 12582912 | bytes 17039360 | tf_op jit(solution)/shard_map/bazi,bazio->bazo/dot_general | solution.py:82
  163.5 15.9 %fusion.154 = f32[32,2,16,1,32]{4,3,2,1,0:T(1,128)S(1)} fusion(f32[32,2,16,2,32,32]{5,4,3,2,1,0:T(8,128)} %param.10, f32[32,2,16,32,1]{3,2,0,1,4:T(8,128)S(1)} %reshape.87), kind=kOutput, calls=%fused_computation.188 | convolution fusion | flops 12582912 | bytes 17039360 | tf_op jit(solution)/shard_map/bazi,bazio->bazo/dot_general | solution.py:82
  179.9 15.9 %fusion.156 = f32[32,2,16,1,32]{4,3,2,1,0:T(1,128)S(1)} fusion(f32[32,2,16,2,32,32]{5,4,3,2,1,0:T(8,128)} %param.10, f32[32,2,16,32,1]{3,2,0,1,4:T(8,128)S(1)} %reshape.85), kind=kOutput, calls=%fused_computation.190 | convolution fusion | flops 12582912 | bytes 17039360 | tf_op jit(solution)/shard_map/bazi,bazio->bazo/dot_general | solution.py:82
  195.9 16.3 %fusion.150 = f32[32,2,16,1,32]{4,3,2,1,0:T(1,128)S(1)} fusion(f32[32,2,16,2,32,32]{5,4,3,2,1,0:T(8,128)} %param.10, f32[32,2,16,32,1]{3,2,0,1,4:T(8,128)S(1)} %reshape.85), kind=kOutput, calls=%fused_computation.184 | convolution fusion | flops 12582912 | bytes 17039360 | tf_op jit(solution)/shard_map/bazi,bazio->bazo/dot_general | solution.py:82
  215.2 3.5 %all-to-all-start.2 = ((f32[2,32,2,512]{3,0,2,1:T(2,128)}), f32[2,32,2,512]{3,0,2,1:T(2,128)S(1)}, u32[]{:S(2)}, u32[]{:S(2)}) async-start(f32[2,32,2,512]{3,0,2,1:T(2,128)} %copy.37), calls=%async_computation.2 | async-start | bytes 524288 | tf_op jit(solution)/shard_map/all_to_all | solution.py:142
  224.7 5.3 %pad.8 = f32[4,34,66,32]{3,2,0,1:T(8,128)} pad(f32[4,34,64,32]{3,2,0,1:T(8,128)} %reshape.60, f32[]{:T(128)} %constant.66.clone.1), padding=0_0x0_0x1_1x0_0 | pad | bytes 2263044 | tf_op jit(solution)/shard_map/jit(_pad)/pad | solution.py:61
  232.6 6.0 %all-to-all-start.3 = ((f32[32,2,2,512]{3,1,2,0:T(2,128)}), f32[32,2,2,512]{3,1,2,0:T(2,128)}, u32[]{:S(2)}, u32[]{:S(2)}) async-start(f32[32,2,2,512]{3,1,2,0:T(2,128)} %copy.39), calls=%async_computation.3 | async-start | bytes 524288 | tf_op jit(solution)/shard_map/all_to_all | solution.py:146
  238.7 78.7 %while.21 = (s32[]{:T(128)}, f32[2,32,64,32]{2,3,1,0:T(8,128)S(1)}, s32[2]{0:T(128)S(1)}, f32[4,34,66,32]{3,2,0,1:T(8,128)}, f32[3,3,96,32]{2,3,1,0:T(8,128)S(1)...) while((s32[]{:T(128)}, f32[2,32,64,32]{2,3,1,0:T(8,128)S(1)}, s32[2]{0:T(128)S(1)}, ...), condition=%wide.region_3.4_spmd, body=%wide.region_2.3_spmd.sunk | while | flops 683540480 | bytes 54296804 | solution.py:78
  241.7 5.2 %dynamic-slice_bitcast_fusion.21 = (f32[32,66,32]{2,1,0:T(8,128)S(1)}, f32[32,66,32]{2,1,0:T(8,128)S(1)}, f32[32,66,32]{2,1,0:T(8,128)S(1)}, f32[32,66,32]{2,1,0...) fusion(f32[4,34,66,32]{3,2,0,1:T(8,128)} %get-tuple-element.464, ...), kind=kLoop, calls=%fused_computation.102.clone.1 | loop fusion | bytes 4866068 | tf_op jit(solution)/shard_map/while/body/eval_jaxpr/squeeze | solution.py:69
  257.9 3.1 convolution_add_fusion.43
  264.8 3.1 convolution_add_fusion.45
  271.7 3.1 convolution_add_fusion.47
  280.8 5.4 %dynamic-slice_bitcast_fusion.21 = (f32[32,66,32]{2,1,0:T(8,128)S(1)}, f32[32,66,32]{2,1,0:T(8,128)S(1)}, f32[32,66,32]{2,1,0:T(8,128)S(1)}, f32[32,66,32]{2,1,0...) fusion(f32[4,34,66,32]{3,2,0,1:T(8,128)} %get-tuple-element.464, ...), kind=kLoop, calls=%fused_computation.102.clone.1 | loop fusion | bytes 4866068 | tf_op jit(solution)/shard_map/while/body/eval_jaxpr/squeeze | solution.py:69
  290.3 3.1 convolution_add_fusion.41
  297.2 3.1 convolution_add_fusion.43
  311.0 3.1 convolution_add_fusion.47
  321.8 4.1 %fusion.175 = f32[2,32,64,32]{2,3,1,0:T(8,128)S(1)} fusion(f32[2,32,64,32]{2,3,1,0:T(8,128)S(1)} %copy-done.3, f32[64,2,32,32]{0,3,2,1:T(8,128)S(1)} %fusion.190, f32[2,32,2,16,32]{4,3,1,0,2:T(8,128)S(1)} %reshape.56, f32[32]{0:T(128)S(1)} %copy-done.7, f32[16]{0:T(128)S(1)} %copy-done.6), kind=kOutput, calls=%fused_computation.228 | convolution fusion | flops 33963008 | bytes 3146752 | tf_op jit(solution)/shard_map/xykc,kz->xyzc/dot_general | solution.py:153
  (158 shorter events, 139.2 us)
Async XLA Ops:
  0.0 6.3 %copy-start = (f32[2,32,2048]{2,1,0:T(8,128)S(1)}, f32[2,32,2048]{2,1,0:T(8,128)}, u32[]{:S(2)}) copy-start(f32[2,32,2048]{2,1,0:T(8,128)} %param.9) | copy-start | bytes 1572868
  1.9 8.0 %collective-permute-start = (f32[1,32,2048]{2,1,0:T(8,128)}, f32[1,32,2048]{2,1,0:T(8,128)}, u32[]{:S(2)}, u32[]{:S(2)}) collective-permute-start(f32[1,32,2048]{2,1,0:T(8,128)} %get-tuple-element.204), channel_id=1, source_target_pairs={{0,1},{1,2},{2,3},{3,4},{4,5},{5,6},{6,7},{7,8},{8,9},{9,10},{10,1... | collective-permute-start | bytes 786440 | tf_op jit(solution)/shard_map/ppermute | solution.py:26
  5.0 6.0 %collective-permute-start.1 = (f32[1,32,2048]{2,1,0:T(8,128)}, f32[1,32,2048]{2,1,0:T(8,128)}, u32[]{:S(2)}, u32[]{:S(2)}) collective-permute-start(f32[1,32,2048]{2,1,0:T(8,128)} %get-tuple-element.203), channel_id=1, source_target_pairs={{1,0},{2,1},{3,2},{4,3},{5,4},{6,5},{7,6},{8,7},{9,8},{10,9},{11,1... | collective-permute-start | bytes 786440 | tf_op jit(solution)/shard_map/ppermute | solution.py:28
  10.9 12.7 %copy-start.4 = (f32[3,3,3,32,32]{4,3,2,1,0:T(8,128)S(1)}, f32[3,3,3,32,32]{4,3,2,1,0:T(8,128)}, u32[]{:S(2)}) copy-start(f32[3,3,3,32,32]{4,3,2,1,0:T(8,128)} %param.11) | copy-start | bytes 331780
  12.1 11.7 %collective-permute-start.3 = (f32[4,1,2048]{2,1,0:T(1,128)S(1)}, f32[4,1,2048]{2,1,0:T(1,128)S(1)}, u32[]{:S(2)}, u32[]{:S(2)}) collective-permute-start(f32[4,1,2048]{2,1,0:T(1,128)S(1)} %get-tuple-element.202), channel_id=1, source_target_pairs={} | collective-permute-start | bytes 98312 | tf_op jit(solution)/shard_map/ppermute | solution.py:28
  12.7 11.1 %collective-permute-start.2 = (f32[4,1,2048]{2,1,0:T(1,128)S(1)}, f32[4,1,2048]{2,1,0:T(1,128)S(1)}, u32[]{:S(2)}, u32[]{:S(2)}) collective-permute-start(f32[4,1,2048]{2,1,0:T(1,128)S(1)} %get-tuple-element.201), channel_id=1, source_target_pairs={} | collective-permute-start | bytes 98312 | tf_op jit(solution)/shard_map/ppermute | solution.py:26
  14.2 111.0 %all-to-all-start = ((f32[2,32,2,512]{3,0,2,1:T(2,128)}), f32[2,32,2,512]{3,0,2,1:T(2,128)}, u32[]{:S(2)}, u32[]{:S(2)}) async-start(f32[2,32,2,512]{3,0,2,1:T(2,128)} %pad_maximum_fusion.2), calls=%async_computation | async-start | bytes 524288 | tf_op jit(solution)/shard_map/all_to_all | solution.py:109
  117.3 18.9 %collective-permute-start.4 = (f32[1,32,2048]{2,1,0:T(8,128)S(1)}, f32[1,32,2048]{2,1,0:T(8,128)}, u32[]{:S(2)}, u32[]{:S(2)}) collective-permute-start(f32[1,32,2048]{2,1,0:T(8,128)S(1)} %slice.349), channel_id=1, source_target_pairs={{0,1},{1,2},{2,3},{3,4},{4,5},{5,6},{6,7},{7,8},{8,9},{9,10},{10,1... | collective-permute-start | bytes 786440 | tf_op jit(solution)/shard_map/ppermute | solution.py:26
  123.9 13.3 %collective-permute-start.5 = (f32[1,32,2048]{2,1,0:T(8,128)S(1)}, f32[1,32,2048]{2,1,0:T(8,128)S(1)}, u32[]{:S(2)}, u32[]{:S(2)}) collective-permute-start(f32[1,32,2048]{2,1,0:T(8,128)S(1)} %slice.351), channel_id=1, source_target_pairs={{1,0},{2,1},{3,2},{4,3},{5,4},{6,5},{7,6},{8,7},{9,8},{10,9},{11,1... | collective-permute-start | bytes 786440 | tf_op jit(solution)/shard_map/ppermute | solution.py:28
  127.4 9.7 %copy-start.1 = (f32[2,32,2048]{2,1,0:T(8,128)S(1)}, f32[2,32,2048]{2,1,0:T(8,128)}, u32[]{:S(2)}) copy-start(f32[2,32,2048]{2,1,0:T(8,128)} %reshape.59) | copy-start | bytes 1572868
  128.7 17.4 %all-to-all-start.1 = ((f32[32,2,2,512]{3,1,2,0:T(2,128)}), f32[32,2,2,512]{3,1,2,0:T(2,128)S(1)}, u32[]{:S(2)}, u32[]{:S(2)}) async-start(f32[32,2,2,512]{3,1,2,0:T(2,128)} %copy.35), calls=%async_computation.1 | async-start | bytes 524288 | tf_op jit(solution)/shard_map/all_to_all | solution.py:113
  213.5 7.1 %copy-start.5 = (f32[3,3,3,32,32]{4,3,2,1,0:T(8,128)S(1)}, f32[3,3,3,32,32]{4,3,2,1,0:T(8,128)}, u32[]{:S(2)}) copy-start(f32[3,3,3,32,32]{4,3,2,1,0:T(8,128)} %param.12) | copy-start | bytes 331780
  215.2 14.9 %all-to-all-start.2 = ((f32[2,32,2,512]{3,0,2,1:T(2,128)}), f32[2,32,2,512]{3,0,2,1:T(2,128)S(1)}, u32[]{:S(2)}, u32[]{:S(2)}) async-start(f32[2,32,2,512]{3,0,2,1:T(2,128)} %copy.37), calls=%async_computation.2 | async-start | bytes 524288 | tf_op jit(solution)/shard_map/all_to_all | solution.py:142
  218.8 2.0 collective-permute-start.7
  219.4 1.4 collective-permute-start.6
  232.6 84.9 %all-to-all-start.3 = ((f32[32,2,2,512]{3,1,2,0:T(2,128)}), f32[32,2,2,512]{3,1,2,0:T(2,128)}, u32[]{:S(2)}, u32[]{:S(2)}) async-start(f32[32,2,2,512]{3,1,2,0:T(2,128)} %copy.39), calls=%async_computation.3 | async-start | bytes 524288 | tf_op jit(solution)/shard_map/all_to_all | solution.py:146
  317.5 1.0 copy-start.2
  317.5 2.4 copy-start.6
  319.4 2.3 copy-start.7
  319.9 1.9 copy-start.3
where the time goes:
time: 335 us; the launch traced here: 328 us
  matrix products  190 us (57%)
  local copies, waits for them, and re-layouts  77.6 us (23%)
  starting transfers between devices  37.6 us (11%)
  loops' own time  9.4 us (3%)
  waiting for transfers between devices  8.95 us (3%)
  other arithmetic  4.13 us (1%)
    dot_general x36, matrix products, plane(): jnp.einsum('yzi,io->yzo', stacked, kernel[shift_x, shift_y], precision=HI...  112 us
    dot_general x4, matrix products, mode_mix(): return jnp.einsum('bazi,bazio->bazo', inputs, matrix, precision=HIGHEST)  64.1 us
    squeeze x4, local copies, waits for them, and re-layouts, plane(): windowed = slab[shift_x, shift_y:shift_y + extent_y]  21.2 us
    slice x20, local copies, waits for them, and re-layouts, plane(): windowed[:, shift_z:shift_z + NZ]  11.9 us
    pad x2, local copies, waits for them, and re-layouts, convolve(): volume = jnp.pad(volume, ((0, 0), (0, 0), (1, 1), (0, 0)))  10.7 us
    another operation x2, loops' own time, convolve(): return lax.map(plane, jnp.arange(extent_x, dtype=jnp.int32))  9.4 us
    all_to_all x1, starting transfers between devices, body(): lax.all_to_all(z_spectrum, 'gx', split_axis=1, concat_axis=0, tiled=True)  9.39 us
    all_to_all x1, waiting for transfers between devices, body(): lax.all_to_all(kept_modes, 'gx', split_axis=0, concat_axis=1, tiled=True)  8.91 us
  transfers between devices with their start and end apart: 12, of which 1 were waited for; matrix products, arithmetic and copies ran while one was open for 57% of the time, Pallas kernels for 0%

commit v1 on v0

--- a/solution.py
+++ b/solution.py
@@ -3,6 +3,8 @@
 import jax
 import jax.numpy as jnp
 from jax import lax
+from jax.experimental import pallas as pl
+from jax.experimental.pallas import tpu as pltpu
 from jax.sharding import PartitionSpec as P
 
 CH = 32
@@ -13,6 +15,7 @@
 
 
 HIGHEST = lax.Precision.HIGHEST
+HIGH = lax.Precision.HIGH
 
 
 def with_halo(cells, sides, width):
@@ -163,6 +166,272 @@
     return result.reshape(cells_x, cells_y, merged_width)
 
 
+LANES = 256
+STEP = LANES // CH
+BLOCKS = NZ // STEP
+DEPTH = 4 * LANES
+
+
+def split_bf16(value):
+    high = value.astype(jnp.bfloat16)
+    low = (value - high.astype(jnp.float32)).astype(jnp.bfloat16)
+    return high, low
+
+
+def erf(value):
+    value = jnp.clip(value, -3.832506856900711, 3.832506856900711)
+    square = value * value
+    top = jnp.float32(0.00022905065861350646)
+    for term in (0.0034082910107109506, 0.050955695062380861, 0.18520832239976145, 1.128379143519084):
+        top = top * square + term
+    bottom = jnp.float32(-1.1791602954361697e-7)
+    for term in (0.000023547966471313185, 0.0010179625278914885, 0.014070470171167667, 0.11098505178285362, 0.49746925110067538, 1.0):
+        bottom = bottom * square + term
+    return value * top / bottom
+
+
+def gelu(value):
+    return value * (1.0 + erf(value * (0.5**0.5))) * 0.5
+
+
+def conv_kernel(
+    body_ref, below_ref, above_ref, tiled_ref, out_ref, b_high, b_low, a_high, a_low, hidden
+):
+    cells_x, cells_y, _ = body_ref.shape
+    place = lax.axis_index("gx")
+    last = lax.axis_size("gx") - 1
+    lane_block = lax.broadcasted_iota(jnp.int32, (CH, LANES), 1) // CH
+
+    def build_weights(which):
+        def per_shift(dx, carry):
+            zero = jnp.zeros((CH, LANES), jnp.float32)
+
+            def put(row, value):
+                high, low = split_bf16(value)
+                b_high[dx, row : row + CH, :] = high
+                b_low[dx, row : row + CH, :] = low
+
+            for dy in range(3):
+                taps = [tiled_ref[which, dx * 9 + dy * 3 + e] for e in range(3)]
+                for i in range(STEP):
+                    row = zero
+                    for e in range(3):
+                        row = jnp.where(lane_block == i + 1 - e, taps[e], row)
+                    put(dy * LANES + i * CH, row)
+                following = jnp.where(lane_block == STEP - 1, taps[2], 0.0)
+                previous = jnp.where(lane_block == 0, taps[0], 0.0)
+                offsets = ((0, 96), (64, 32), (128, 224))[dy]
+                put(3 * LANES + offsets[0], following)
+                put(3 * LANES + offsets[1], previous)
+            put(3 * LANES + 160, zero)
+            put(3 * LANES + 192, zero)
+            return carry
+
+        lax.fori_loop(0, 3, per_shift, 0)
+
+    row_y = lax.broadcasted_iota(jnp.int32, (cells_y, 128), 0)
+    lane = lax.broadcasted_iota(jnp.int32, (cells_y, 128), 1)
+    row_wide = lax.broadcasted_iota(jnp.int32, (cells_y, LANES), 0)
+
+    def shifted(value, dy, rows):
+        if dy == 1:
+            return value
+        if dy == 0:
+            return jnp.where(rows == 0, 0.0, pltpu.roll(value, 1, 0))
+        return jnp.where(rows == cells_y - 1, 0.0, pltpu.roll(value, cells_y - 1, 0))
+
+    def build_plane(slot, fetch):
+        for b in range(BLOCKS):
+            rows = slice(b * cells_y, (b + 1) * cells_y)
+
+            def put(column, value):
+                high, low = split_bf16(value)
+                width = value.shape[1]
+                a_high[slot, rows, column : column + width] = high
+                a_low[slot, rows, column : column + width] = low
+
+            main = fetch(b * LANES, LANES)
+            edge = jnp.zeros((cells_y, 128), jnp.float32)
+            if b > 0:
+                edge = jnp.where(lane >= 96, fetch(b * LANES - 128, 128), edge)
+            if b < BLOCKS - 1:
+                edge = jnp.where(lane < CH, fetch((b + 1) * LANES, 128), edge)
+            for dy in range(3):
+                put(dy * LANES, shifted(main, dy, row_wide))
+            put(3 * LANES, shifted(edge, 0, row_y) + pltpu.roll(edge, 64, 1))
+            put(3 * LANES + 128, shifted(edge, 2, row_y))
+
+    def multiply(plane):
+        total = jnp.zeros((BLOCKS * cells_y, LANES), jnp.float32)
+        for dx in range(3):
+            left_high = a_high[plane + dx]
+            left_low = a_low[plane + dx]
+            right_high = b_high[dx]
+            total += jnp.dot(left_high, right_high, preferred_element_type=jnp.float32)
+            total += jnp.dot(left_high, b_low[dx], preferred_element_type=jnp.float32)
+            total += jnp.dot(left_low, right_high, preferred_element_type=jnp.float32)
+        return total
+
+    build_weights(0)
+
+    def from_ref(ref, x, keep):
+        def fetch(column, width):
+            value = ref[x, :, column : column + width]
+            return value if keep is None else jnp.where(keep, value, 0.0)
+
+        return fetch
+
+    def outer(x, carry):
+        build_plane(x, from_ref(below_ref, x, place > 0))
+        build_plane(cells_x + 2 + x, from_ref(above_ref, x, place < last))
+        return carry
+
+    def inner(x, carry):
+        build_plane(x + 2, from_ref(body_ref, x, None))
+        return carry
+
+    lax.fori_loop(0, 2, outer, 0)
+    lax.fori_loop(0, cells_x, inner, 0)
+
+    def first(plane, carry):
+        inside = jnp.logical_and(
+            jnp.logical_or(plane > 0, place > 0),
+            jnp.logical_or(plane < cells_x + 1, place < last),
+        )
+        hidden[plane] = jnp.where(inside, gelu(multiply(plane)), 0.0)
+        return carry
+
+    lax.fori_loop(0, cells_x + 2, first, 0)
+    build_weights(1)
+
+    def rebuild(plane, carry):
+        def fetch(column, width):
+            b = column // LANES
+            start = column - b * LANES
+            return hidden[plane, b * cells_y : (b + 1) * cells_y, start : start + width]
+
+        build_plane(plane, fetch)
+        return carry
+
+    lax.fori_loop(0, cells_x + 2, rebuild, 0)
+
+    def second(plane, carry):
+        total = multiply(plane)
+        for b in range(BLOCKS):
+            out_ref[plane, :, b * LANES : (b + 1) * LANES] = total[b * cells_y : (b + 1) * cells_y]
+        return carry
+
+    lax.fori_loop(0, cells_x, second, 0)
+
+
+def two_convolutions(field, conv_first, conv_second):
+    cells_x, cells_y, merged_width = field.shape
+    count = lax.axis_size("gx")
+    pairs = [(i, i + 1) for i in range(count - 1)]
+    below = lax.ppermute(field[cells_x - 2 :], "gx", pairs)
+    above = lax.ppermute(field[:2], "gx", [(j, i) for i, j in pairs])
+    tiled = jnp.tile(jnp.stack([conv_first, conv_second]).reshape(2, 27, CH, CH), (1, 1, 1, STEP))
+    rows = BLOCKS * cells_y
+    vmem = pl.BlockSpec(memory_space=pltpu.VMEM)
+    flops = 2 * 3 * 3 * (2 * cells_x + 2) * rows * DEPTH * LANES
+    return pl.pallas_call(
+        conv_kernel,
+        out_shape=jax.ShapeDtypeStruct(field.shape, jnp.float32),
+        in_specs=[vmem] * 4,
+        out_specs=vmem,
+        scratch_shapes=[
+            pltpu.VMEM((3, DEPTH, LANES), jnp.bfloat16),
+            pltpu.VMEM((3, DEPTH, LANES), jnp.bfloat16),
+            pltpu.VMEM((cells_x + 4, rows, DEPTH), jnp.bfloat16),
+            pltpu.VMEM((cells_x + 4, rows, DEPTH), jnp.bfloat16),
+            pltpu.VMEM((cells_x + 2, rows, LANES), jnp.float32),
+        ],
+        cost_estimate=pl.CostEstimate(flops=flops, bytes_accessed=8 * field.size, transcendentals=0),
+        compiler_params=pltpu.CompilerParams(vmem_limit_bytes=28 * 2**20),
+    )(field, below, above, tiled)
+
+
+def mix_kernel(modes_ref, weight_ref, out_ref):
+    rows, owned_x, depth = weight_ref.shape[:3]
+    mode = 0
+    for y in range(rows):
+        for x in range(owned_x):
+            for k in range(depth):
+                real = jnp.broadcast_to(modes_ref[0, 0, :, mode : mode + 1], (CH, CH))
+                imag = jnp.broadcast_to(modes_ref[0, 1, :, mode : mode + 1], (CH, CH))
+                weight_real = weight_ref[y, x, k, 0]
+                weight_imag = weight_ref[y, x, k, 1]
+                out_ref[0, 0, mode : mode + 1, :] = jnp.sum(
+                    real * weight_real - imag * weight_imag, axis=0, keepdims=True
+                )
+                out_ref[0, 1, mode : mode + 1, :] = jnp.sum(
+                    real * weight_imag + imag * weight_real, axis=0, keepdims=True
+                )
+                mode += 1
+
+
+def mix_modes(complex_parts, spectral):
+    rows, owned_x = spectral.shape[:2]
+    per = 2
+    count = per * owned_x * MZ
+    steps = rows // per
+    modes = complex_parts.reshape(steps, per, owned_x, 2, MZ, CH).transpose(0, 3, 5, 1, 2, 4)
+    out = pl.pallas_call(
+        mix_kernel,
+        grid=(steps,),
+        out_shape=jax.ShapeDtypeStruct((steps, 2, count, CH), jnp.float32),
+        in_specs=[
+            pl.BlockSpec((1, 2, CH, count), lambda i: (i, 0, 0, 0)),
+            pl.BlockSpec((per, owned_x, MZ, 2, CH, CH), lambda i: (i, 0, 0, 0, 0, 0)),
+        ],
+        out_specs=pl.BlockSpec((1, 2, count, CH), lambda i: (i, 0, 0, 0)),
+        cost_estimate=pl.CostEstimate(flops=8 * spectral.size, bytes_accessed=16 * spectral.size, transcendentals=0),
+    )(modes.reshape(steps, 2, CH, count), spectral)
+    return out.reshape(steps, 2, per, owned_x, MZ, CH).transpose(0, 2, 3, 1, 4, 5)
+
+
+def complex_table(cos_table, sin_table, sign):
+    top = jnp.stack([cos_table, sign * sin_table], axis=1)
+    bottom = jnp.stack([-sign * sin_table, cos_table], axis=1)
+    return jnp.stack([top, bottom], axis=0)
+
+
+def line_body(field, spectral, conv_first, conv_second, bias):
+    cells_x, cells_y, merged_width = field.shape
+    devices_x = lax.axis_size("gx")
+    extent_x = cells_x * devices_x
+    extent_y = cells_y
+    owned_x = MX // devices_x
+    mode_width = MZ * CH
+    second_branch = two_convolutions(field, conv_first, conv_second)
+    z_index = jnp.arange(MZ, dtype=jnp.int32)
+    z_cos, z_sin = angle_table(z_index, jnp.arange(NZ, dtype=jnp.int32), NZ)
+    volume = field.reshape(cells_x, cells_y, NZ, CH)
+    forward_z = jnp.stack([z_cos, -z_sin])
+    z_spectrum = jnp.einsum("xyzc,rkz->xyrkc", volume, forward_z, precision=HIGH)
+    z_spectrum = z_spectrum.reshape(cells_x, cells_y, 2, mode_width)
+    kept_x = frequency(jnp.arange(MX, dtype=jnp.int32), extent_x, MX)
+    kept_y = frequency(jnp.arange(MY, dtype=jnp.int32), extent_y, MY)
+    x_table = complex_table(*angle_table(kept_x, jnp.arange(extent_x, dtype=jnp.int32), extent_x), 1.0)
+    y_table = complex_table(*angle_table(kept_y, jnp.arange(extent_y, dtype=jnp.int32), extent_y), 1.0)
+    lines = lax.all_to_all(z_spectrum, "gx", split_axis=1, concat_axis=0, tiled=True)
+    kept = jnp.einsum("akbx,xybm->kyam", x_table, lines, precision=HIGH)
+    x_modes = lax.all_to_all(kept, "gx", split_axis=0, concat_axis=1, tiled=True)
+    all_modes = jnp.einsum("akby,xybm->kxam", y_table, x_modes, precision=HIGH)
+    mixed = mix_modes(all_modes, spectral).reshape(MY, owned_x, 2, mode_width)
+    y_cells = jnp.einsum("bkay,kxbm->xyam", y_table, mixed, precision=HIGH)
+    lines = lax.all_to_all(y_cells, "gx", split_axis=1, concat_axis=0, tiled=True)
+    lines = jnp.einsum("bkax,kybm->xyam", x_table, lines, precision=HIGH)
+    planes = lax.all_to_all(lines, "gx", split_axis=0, concat_axis=1, tiled=True)
+    weights = jnp.where(z_index == 0, 1.0, 2.0).astype(jnp.float32) / (extent_x * extent_y * NZ)
+    back_z = jnp.stack([z_cos * weights[:, None], -z_sin * weights[:, None]])
+    spectral_part = jnp.einsum(
+        "xyrkc,rkz->xyzc", planes.reshape(cells_x, cells_y, 2, MZ, CH), back_z, precision=HIGH
+    )
+    total = spectral_part.reshape(field.shape) + second_branch + jnp.tile(bias, NZ)
+    return jax.nn.gelu(total, approximate=False)
+
+
 def solution(mesh):
     in_specs = (
         P(("groups", "gx"), "gy", None),
@@ -172,4 +441,5 @@
         P(),
     )
     out_specs = P(("groups", "gx"), "gy", None)
-    return jax.shard_map(body, mesh=mesh, in_specs=in_specs, out_specs=out_specs, check_vma=False)
+    chosen = line_body if mesh.shape["gy"] == 1 else body
+    return jax.shard_map(chosen, mesh=mesh, in_specs=in_specs, out_specs=out_specs, check_vma=False)

time: 335 us -> 116 us (0.35); the launches traced: 328 us -> 115 us
  matrix products: 190 us -> 3.83 us
  local copies, waits for them, and re-layouts: 77.6 us -> 28.9 us
  Pallas kernels: 0 us -> 33.7 us
  starting transfers between devices: 37.6 us -> 23.1 us
  blocking collectives: 0 us -> 12.7 us
  loops' own time: 9.4 us -> 0 us
    dot_general x60 -> x6, matrix products: 190 us -> 3.83 us  [the longest x1 1.25 us: line_body(): lines = jnp.einsum('bkax,kybm->xyam', x_table, lines, precision=HIGH)]
    pallas_call x0 -> x2, Pallas kernels: none -> 33.7 us  [the longest x1 21.3 us: mix_modes(): pl.pallas_call(mix_kernel, grid=(steps,), out_shape=jax.ShapeDtypeStruct(...]
    squeeze x8 -> x0, local copies, waits for them, and re-layouts: 22 us -> none  [the longest x4 21.2 us: plane(): windowed = slab[shift_x, shift_y:shift_y + extent_y]]
    slice x28 -> x0, local copies, waits for them, and re-layouts: 18.7 us -> none  [the longest x20 11.9 us: plane(): windowed[:, shift_z:shift_z + NZ]]
    all_to_all x0 -> x1, blocking collectives: none -> 12.7 us  [line_body(): lax.all_to_all(kept, 'gx', split_axis=0, concat_axis=1, tiled=True)]
    pad x2 -> x0, local copies, waits for them, and re-layouts: 10.7 us -> none  [convolve(): volume = jnp.pad(volume, ((0, 0), (0, 0), (1, 1), (0, 0)))]
    another operation x2 -> x0, loops' own time: 9.4 us -> none  [convolve(): return lax.map(plane, jnp.arange(extent_x, dtype=jnp.int32))]
    ppermute x8 -> x2, starting transfers between devices: 11.2 us -> 3.45 us  [the longest x1 2.16 us: two_convolutions(): below = lax.ppermute(field[cells_x - 2:], 'gx', pairs)]
  transfers between devices with their start and end apart: 12 -> 5, of which waited for: 1 -> 1; matrix products, arithmetic and copies ran while one was open for 57% -> 13% of each run, Pallas kernels for 0% -> 11%
where the time goes in v1:
time: 116 us; the launch traced here: 115 us
  Pallas kernels  33.7 us (29%)
  local copies, waits for them, and re-layouts  28.9 us (25%)
  starting transfers between devices  23.1 us (20%)
  blocking collectives  12.7 us (11%)
  waiting for transfers between devices  9.83 us (8%)
  matrix products  3.83 us (3%)
  other arithmetic  2.33 us (2%)
    pallas_call x1, Pallas kernels, mix_modes(): pl.pallas_call(mix_kernel, grid=(steps,), out_shape=jax.ShapeDtypeStruct(...  21.3 us
    all_to_all x1, blocking collectives, line_body(): lax.all_to_all(kept, 'gx', split_axis=0, concat_axis=1, tiled=True)  12.7 us
    pallas_call x1, Pallas kernels, two_convolutions(): pl.pallas_call(conv_kernel, out_shape=jax.ShapeDtypeStruct(field.shape, j...  12.4 us
    all_to_all x1, waiting for transfers between devices, line_body(): lax.all_to_all(z_spectrum, 'gx', split_axis=1, concat_axis=0, tiled=True)  9.82 us
    another operation x2, local copies, waits for them, and re-layouts, two_convolutions(): jnp.tile(jnp.stack([conv_first, conv_second]).reshape(2, 27, CH, CH), (1,...  8.46 us
    all_to_all x1, starting transfers between devices, line_body(): lax.all_to_all(lines, 'gx', split_axis=0, concat_axis=1, tiled=True)  8.09 us
    all_to_all x1, starting transfers between devices, line_body(): lax.all_to_all(z_spectrum, 'gx', split_axis=1, concat_axis=0, tiled=True)  7.41 us
    all_to_all x1, starting transfers between devices, line_body(): lax.all_to_all(y_cells, 'gx', split_axis=1, concat_axis=0, tiled=True)  4.19 us
  transfers between devices with their start and end apart: 5, of which 1 were waited for; matrix products, arithmetic and copies ran while one was open for 13% of the time, Pallas kernels for 11%

profile of v1, /device:TPU:0, one launch (start us, length us, event | category | flops | bytes accessed | tf_op | source)
XLA Modules:
  0.0 114.7 jit_solution(13690079002681043232)
XLA Ops:
  0.1 1.8 %reshape.244 = f32[2,32,64,32]{3,2,1,0:T(8,128)S(1)} reshape(f32[2,32,2048]{2,1,0:T(8,128)} %body_ref.1) | data formatting | bytes 1048576 | tf_op jit(solution)/shard_map/reshape | solution.py:409
  1.9 0.6 fusion.2
  2.5 0.4 reshape.245
  2.9 0.9 copy.28
  3.8 7.4 %all-to-all-start = ((f32[2,32,2,512]{3,0,2,1:T(2,128)}), f32[2,32,2,512]{3,0,2,1:T(2,128)S(1)}, u32[]{:S(2)}, u32[]{:S(2)}) async-start(f32[2,32,2,512]{3,0,2,1:T(2,128)} %copy.28), calls=%async_computation | async-start | bytes 524288 | tf_op jit(solution)/shard_map/all_to_all | solution.py:417
  11.4 9.8 %all-to-all-done = f32[2,32,2,512]{3,0,2,1:T(2,128)S(1)} async-done(((f32[2,32,2,512]{3,0,2,1:T(2,128)}), f32[2,32,2,512]{3,0,2,1:T(2,128)S(1)}, u32[]{:S(2)}, u32[]{:S(2)}) %all-to-all-start) | async-done | bytes 262176 | tf_op jit(solution)/shard_map/all_to_all | solution.py:417
  21.5 0.3 convolution_bitcast_fusion.4
  22.0 12.7 %all_to_all.69 = f32[32,2,2,512]{3,2,1,0:T(2,128)S(1)} all-to-all(f32[32,2,2,512]{3,2,1,0:T(2,128)S(1)} %copy.30), channel_id=1, replica_groups=mesh['groups'=2,'gx'=16,'gy'=1] {'gx'}, dimensions={0} | all-to-all | bytes 524288 | tf_op jit(solution)/shard_map/all_to_all | solution.py:419
  35.8 1.1 copy.33.modes_ref
  36.9 21.3 %shard_map.55 = f32[16,2,64,32]{3,2,1,0:T(8,128)} custom-call(f32[16,2,32,64]{3,2,1,0:T(8,128)} %copy.33.modes_ref, f32[32,2,16,2,32,32]{5,4,3,2,1,0:T(8,128)} %weight_ref.1), custom_call_target="tpu_custom_call" | custom-call | flops 16777216 | bytes 33554432 | tf_op jit(solution)/shard_map/pallas_call | solution.py:379
  58.2 1.5 %copy.34 = f32[16,2,2,2,16,32]{5,4,1,0,3,2:T(8,128)S(1)} copy(f32[16,2,2,2,16,32]{5,4,2,1,3,0:T(8,128)} %bitcast.123) | data formatting | bytes 524288 | tf_op jit(solution)/shard_map/transpose | solution.py:390
  59.7 0.4 reshape.259
  60.4 0.9 copy.36
  61.3 4.2 %all-to-all-start.2 = ((f32[2,32,2,512]{3,2,0,1:T(2,128)}), f32[2,32,2,512]{3,2,0,1:T(2,128)}, u32[]{:S(2)}, u32[]{:S(2)}) async-start(f32[2,32,2,512]{3,2,0,1:T(2,128)} %copy.36), calls=%async_computation.2 | async-start | bytes 524288 | tf_op jit(solution)/shard_map/all_to_all | solution.py:423
  65.5 2.2 %collective-permute-start = (f32[2,32,2048]{2,1,0:T(8,128)S(1)}, f32[2,32,2048]{2,1,0:T(8,128)S(1)}, u32[]{:S(2)}, u32[]{:S(2)}) collective-permute-start(f32[2,32,2048]{2,1,0:T(8,128)S(1)} %copy-done), channel_id=1, source_target_pairs={{0,1},{1,2},{2,3},{3,4},{4,5},{5,6},{6,7},{7,8},{8,9},{9,10},{10,1... | collective-permute-start | bytes 1572872 | tf_op jit(solution)/shard_map/ppermute | solution.py:331
  67.7 1.3 %collective-permute-start.1 = (f32[2,32,2048]{2,1,0:T(8,128)S(1)}, f32[2,32,2048]{2,1,0:T(8,128)S(1)}, u32[]{:S(2)}, u32[]{:S(2)}) collective-permute-start(f32[2,32,2048]{2,1,0:T(8,128)S(1)} %copy-done), channel_id=1, source_target_pairs={{1,0},{2,1},{3,2},{4,3},{5,4},{6,5},{7,6},{8,7},{9,8},{10,9},{11,1... | collective-permute-start | bytes 1572872 | tf_op jit(solution)/shard_map/ppermute | solution.py:332
  69.1 3.4 %tile.17 = f32[2,27,32,8,32]{4,3,2,1,0:T(8,128)} broadcast(f32[2,27,32,32]{3,2,1,0:T(8,128)S(1)} %maximum_bitcast_fusion), dimensions={0,1,2,4} | broadcast | bytes 1990656 | tf_op jit(solution)/shard_map/tile | solution.py:333
  72.5 5.0 %tile.18.tiled_ref = f32[2,27,32,256]{3,2,1,0:T(8,128)S(1)} reshape(f32[2,27,32,8,32]{4,3,2,1,0:T(8,128)} %tile.17) | data formatting | bytes 3538944 | tf_op jit(solution)/shard_map/tile | solution.py:333
  77.8 1.8 %copy.66 = f32[2,16,2,2,512]{4,0,1,3,2:T(2,128)} copy(f32[2,16,2,2,512]{4,3,0,2,1:T(2,128)} %bitcast.30) | data formatting | bytes 524288 | tf_op jit(solution)/shard_map/all_to_all | solution.py:423
  79.6 1.8 %reshape.262 = f32[32,2,2,512,1]{3,0,2,1,4:T(8,128)} reshape(f32[16,2,2,2,512]{4,1,0,3,2:T(2,128)} %bitcast.130) | data formatting | bytes 524288 | tf_op jit(solution)/shard_map/all_to_all | solution.py:423
  81.4 1.3 %convolution_bitcast_fusion.1 = f32[32,2,2,512]{3,0,2,1:T(8,128)S(1)} fusion(f32[32,2,2,512,1]{3,0,2,1,4:T(8,128)} %reshape.262, f32[1,32,2,32]{3,1,2,0:T(8,128)S(1)} %get-tuple-element.6, f32[1,32,2,32]{3,1,2,0:T(8,128)S(1)} %get-tuple-element.5), kind=kOutput, calls=%fused_computation.4 | convolution fusion | flops 25169920 | bytes 540672 | tf_op jit(solution)/shard_map/bkax,kybm->xyam/dot_general | solution.py:424
  82.6 0.9 copy.39
  83.5 8.1 %all-to-all-start.3 = ((f32[32,2,2,512]{3,2,1,0:T(2,128)}), f32[32,2,2,512]{3,2,1,0:T(2,128)}, u32[]{:S(2)}, u32[]{:S(2)}) async-start(f32[32,2,2,512]{3,2,1,0:T(2,128)} %copy.39), calls=%async_computation.3 | async-start | bytes 524288 | tf_op jit(solution)/shard_map/all_to_all | solution.py:425
  91.7 0.8 copy-done.1
  92.4 1.0 copy-done.2
  93.5 12.4 %shard_map.56 = f32[2,32,2048]{2,1,0:T(8,128)S(1)} custom-call(f32[2,32,2048]{2,1,0:T(8,128)S(1)} %copy-done, f32[2,32,2048]{2,1,0:T(8,128)S(1)} %collective-permute-done.below_ref, f32[2,32,2048]{2,1,0:T(8,128)S(1)} %copy-done.2, f32[2,27,32,256]{3,2,1,0:T(8,128)S(1)} %tile.18.tiled_ref), custom_call_target="tpu_custom_call" | custom-call | flops 7247757312 | bytes 1048576 | tf_op jit(solution)/shard_map/pallas_call | solution.py:337
  105.9 1.0 copy.65
  106.9 0.4 reshape.250
  107.3 1.0 convolution_bitcast_fusion
  108.3 2.0 %copy.41 = f32[2,32,64,32]{3,2,1,0:T(8,128)} copy(f32[2,32,64,32]{2,3,1,0:T(8,128)S(1)} %convolution_bitcast_fusion) | data formatting | bytes 1048576 | tf_op jit(solution)/shard_map/xyrkc,rkz->xyzc/transpose | solution.py:428
  110.3 2.5 %reshape.251 = f32[2,32,2048]{2,1,0:T(8,128)S(1)} reshape(f32[2,32,64,32]{3,2,1,0:T(8,128)} %copy.41) | data formatting | bytes 1048576 | tf_op jit(solution)/shard_map/reshape | solution.py:431
  112.8 1.9 %fusion.6 = f32[2,32,2048]{2,1,0:T(8,128)} fusion(f32[2,32,2048]{2,1,0:T(8,128)S(1)} %reshape.251, f32[2,32,2048]{2,1,0:T(8,128)S(1)} %shard_map.56, f32[2048]{0:T(1024)S(1)} %add.76), kind=kLoop, calls=%fused_computation.11 | loop fusion | flops 8650752 | bytes 1581056 | tf_op jit(solution)/shard_map/mul | solution.py:432
  (32 shorter events, 2.3 us)
Async XLA Ops:
  3.8 17.4 %all-to-all-start = ((f32[2,32,2,512]{3,0,2,1:T(2,128)}), f32[2,32,2,512]{3,0,2,1:T(2,128)S(1)}, u32[]{:S(2)}, u32[]{:S(2)}) async-start(f32[2,32,2,512]{3,0,2,1:T(2,128)} %copy.28), calls=%async_computation | async-start | bytes 524288 | tf_op jit(solution)/shard_map/all_to_all | solution.py:417
  58.2 7.3 %copy-start = (f32[2,32,2048]{2,1,0:T(8,128)S(1)}, f32[2,32,2048]{2,1,0:T(8,128)}, u32[]{:S(2)}) copy-start(f32[2,32,2048]{2,1,0:T(8,128)} %body_ref.1) | copy-start | bytes 1572868
  58.2 10.8 %copy-start.3 = (f32[3,3,3,32,32]{4,3,2,1,0:T(8,128)S(1)}, f32[3,3,3,32,32]{4,3,2,1,0:T(8,128)}, u32[]{:S(2)}) copy-start(f32[3,3,3,32,32]{4,3,2,1,0:T(8,128)} %param.8) | copy-start | bytes 331780
  58.2 10.8 %copy-start.4 = (f32[3,3,3,32,32]{4,3,2,1,0:T(8,128)S(1)}, f32[3,3,3,32,32]{4,3,2,1,0:T(8,128)}, u32[]{:S(2)}) copy-start(f32[3,3,3,32,32]{4,3,2,1,0:T(8,128)} %param.7) | copy-start | bytes 331780
  61.3 16.4 %all-to-all-start.2 = ((f32[2,32,2,512]{3,2,0,1:T(2,128)}), f32[2,32,2,512]{3,2,0,1:T(2,128)}, u32[]{:S(2)}, u32[]{:S(2)}) async-start(f32[2,32,2,512]{3,2,0,1:T(2,128)} %copy.36), calls=%async_computation.2 | async-start | bytes 524288 | tf_op jit(solution)/shard_map/all_to_all | solution.py:423
  65.5 26.1 %collective-permute-start = (f32[2,32,2048]{2,1,0:T(8,128)S(1)}, f32[2,32,2048]{2,1,0:T(8,128)S(1)}, u32[]{:S(2)}, u32[]{:S(2)}) collective-permute-start(f32[2,32,2048]{2,1,0:T(8,128)S(1)} %copy-done), channel_id=1, source_target_pairs={{0,1},{1,2},{2,3},{3,4},{4,5},{5,6},{6,7},{7,8},{8,9},{9,10},{10,1... | collective-permute-start | bytes 1572872 | tf_op jit(solution)/shard_map/ppermute | solution.py:331
  67.7 23.9 %collective-permute-start.1 = (f32[2,32,2048]{2,1,0:T(8,128)S(1)}, f32[2,32,2048]{2,1,0:T(8,128)S(1)}, u32[]{:S(2)}, u32[]{:S(2)}) collective-permute-start(f32[2,32,2048]{2,1,0:T(8,128)S(1)} %copy-done), channel_id=1, source_target_pairs={{1,0},{2,1},{3,2},{4,3},{5,4},{6,5},{7,6},{8,7},{9,8},{10,9},{11,1... | collective-permute-start | bytes 1572872 | tf_op jit(solution)/shard_map/ppermute | solution.py:332
  72.5 5.1 %copy-start.5 = (f32[32]{0:T(128)S(1)}, f32[32]{0:T(128)}, u32[]{:S(2)}) copy-start(f32[32]{0:T(128)} %param.9) | copy-start | bytes 388
  83.5 22.4 %all-to-all-start.3 = ((f32[32,2,2,512]{3,2,1,0:T(2,128)}), f32[32,2,2,512]{3,2,1,0:T(2,128)}, u32[]{:S(2)}, u32[]{:S(2)}) async-start(f32[32,2,2,512]{3,2,1,0:T(2,128)} %copy.39), calls=%async_computation.3 | async-start | bytes 524288 | tf_op jit(solution)/shard_map/all_to_all | solution.py:425
  91.6 0.8 copy-start.1
  92.4 1.0 copy-start.2

commit v2 on v1

--- a/solution.py
+++ b/solution.py
@@ -1,7 +1,9 @@
+import functools
 import math
 
 import jax
 import jax.numpy as jnp
+import numpy as np
 from jax import lax
 from jax.experimental import pallas as pl
 from jax.experimental.pallas import tpu as pltpu
@@ -194,15 +196,103 @@
     return value * (1.0 + erf(value * (0.5**0.5))) * 0.5
 
 
-def conv_kernel(
-    body_ref, below_ref, above_ref, tiled_ref, out_ref, b_high, b_low, a_high, a_low, hidden
+MESH = pl.DeviceIdType.MESH
+
+
+def block_kernel(
+    count, body_ref, spectral_ref, first_ref, second_ref, bias_ref, z_ref, scale_ref,
+    x_in_ref, y_in_ref, y_out_ref, x_out_ref, out_ref,
+    b_high, b_low, a_high, a_low, hidden, z_high, z_low, weights, modes, mixed, spectrum,
+    below, above, sends, lands, send_sems, land_sems, halo_send, halo_land, weight_sem,
 ):
-    cells_x, cells_y, _ = body_ref.shape
+    cells_x, cells_y, merged_width = body_ref.shape
+    owned_x = spectral_ref.shape[1]
+    mode_width = MZ * CH
+    block = sends.shape[1] // count
     place = lax.axis_index("gx")
-    last = lax.axis_size("gx") - 1
+    last = count - 1
+
+    barrier = pltpu.get_barrier_semaphore()
+    for offset in range(1, count):
+        pl.semaphore_signal(
+            barrier, inc=1, device_id={"gx": lax.rem(place + offset, count)}, device_id_type=MESH
+        )
+    weight_copy = pltpu.make_async_copy(spectral_ref, weights, weight_sem)
+    weight_copy.start()
+
+    def at(index):
+        return pl.ds(pl.multiple_of(index * block, 8), block)
+
+    def exchange(stage):
+        copies = []
+        for offset in [o for k in range(count // 2, 0, -1) for o in sorted({k, count - k})]:
+            peer = lax.rem(place + offset, count)
+            copy = pltpu.make_async_remote_copy(
+                src_ref=sends.at[stage, at(peer)],
+                dst_ref=lands.at[stage, at(place)],
+                send_sem=send_sems.at[stage, offset],
+                recv_sem=land_sems.at[stage, offset],
+                device_id={"gx": peer},
+                device_id_type=MESH,
+            )
+            copy.start()
+            copies.append(copy)
+        lands[stage, at(place), :] = sends[stage, at(place), :]
+        return copies
+
+    def finish(copies):
+        for copy in copies:
+            copy.wait()
+
+    def build_z(z, carry):
+        row = z_ref[pl.ds(z, 1), :]
+        high = row.astype(jnp.bfloat16).astype(jnp.float32)
+        low = row - high
+        lane = lax.broadcasted_iota(jnp.int32, (CH, 2 * mode_width), 1)
+        keep = lane % CH == lax.broadcasted_iota(jnp.int32, (CH, 2 * mode_width), 0)
+        rows = pl.ds(pl.multiple_of(z * CH, CH), CH)
+        z_high[rows, :] = jnp.where(keep, high, 0.0).astype(jnp.bfloat16)
+        z_low[rows, :] = jnp.where(keep, low, 0.0).astype(jnp.bfloat16)
+        return carry
+
+    lax.fori_loop(0, NZ, build_z, 0)
+    data_high, data_low = split_bf16(body_ref[...].reshape(cells_x * cells_y, merged_width))
+    for ri in range(2):
+        columns = slice(ri * mode_width, (ri + 1) * mode_width)
+        part = jnp.dot(data_high, z_high[:, columns], preferred_element_type=jnp.float32)
+        part += jnp.dot(data_high, z_low[:, columns], preferred_element_type=jnp.float32)
+        part += jnp.dot(data_low, z_high[:, columns], preferred_element_type=jnp.float32)
+        for x in range(cells_x):
+            rows = pl.ds(x * 2 + ri, cells_y, stride=2 * cells_x)
+            for q in range(mode_width // 128):
+                lanes = slice(q * 128, (q + 1) * 128)
+                spectrum[q, rows, :] = part[x * cells_y : (x + 1) * cells_y, lanes]
+    for q in range(mode_width // 128):
+        sends[0, :, q * 128 : (q + 1) * 128] = spectrum[q]
+
+    pl.semaphore_wait(barrier, count - 1)
+    copies = exchange(0)
+
+    up = pltpu.make_async_remote_copy(
+        src_ref=body_ref.at[pl.ds(cells_x - 2, 2)], dst_ref=below, send_sem=halo_send.at[0],
+        recv_sem=halo_land.at[0], device_id={"gx": lax.rem(place + 1, count)}, device_id_type=MESH,
+    )
+    down = pltpu.make_async_remote_copy(
+        src_ref=body_ref.at[pl.ds(0, 2)], dst_ref=above, send_sem=halo_send.at[1],
+        recv_sem=halo_land.at[1], device_id={"gx": lax.rem(place + last, count)}, device_id_type=MESH,
+    )
+
+    @pl.when(place < last)
+    def _():
+        up.start()
+
+    @pl.when(place > 0)
+    def _():
+        down.start()
+
     lane_block = lax.broadcasted_iota(jnp.int32, (CH, LANES), 1) // CH
 
-    def build_weights(which):
+    def build_weights(tap_ref):
         def per_shift(dx, carry):
             zero = jnp.zeros((CH, LANES), jnp.float32)
 
@@ -212,7 +302,9 @@
                 b_low[dx, row : row + CH, :] = low
 
             for dy in range(3):
-                taps = [tiled_ref[which, dx * 9 + dy * 3 + e] for e in range(3)]
+                taps = [
+                    jnp.concatenate([tap_ref[dx * 9 + dy * 3 + e]] * STEP, axis=1) for e in range(3)
+                ]
                 for i in range(STEP):
                     row = zero
                     for e in range(3):
@@ -272,26 +364,48 @@
             total += jnp.dot(left_low, right_high, preferred_element_type=jnp.float32)
         return total
 
-    build_weights(0)
-
-    def from_ref(ref, x, keep):
-        def fetch(column, width):
-            value = ref[x, :, column : column + width]
-            return value if keep is None else jnp.where(keep, value, 0.0)
-
-        return fetch
-
-    def outer(x, carry):
-        build_plane(x, from_ref(below_ref, x, place > 0))
-        build_plane(cells_x + 2 + x, from_ref(above_ref, x, place < last))
-        return carry
+    def from_ref(ref, x):
+        return lambda column, width: ref[x, :, column : column + width]
 
     def inner(x, carry):
-        build_plane(x + 2, from_ref(body_ref, x, None))
-        return carry
-
-    lax.fori_loop(0, 2, outer, 0)
+        build_plane(x + 2, from_ref(body_ref, x))
+        return carry
+
+    def lower(x, carry):
+        build_plane(x, from_ref(below, x))
+        return carry
+
+    def upper(x, carry):
+        build_plane(cells_x + 2 + x, from_ref(above, x))
+        return carry
+
+    build_weights(first_ref)
     lax.fori_loop(0, cells_x, inner, 0)
+
+    finish(copies)
+    sends[1] = jnp.dot(x_in_ref[...], lands[0], precision=HIGHEST, preferred_element_type=jnp.float32)
+    copies = exchange(1)
+
+    @pl.when(place < last)
+    def _():
+        up.wait_send()
+        down.wait_recv()
+
+    @pl.when(place == last)
+    def _():
+        above[...] = jnp.zeros_like(above)
+
+    @pl.when(place > 0)
+    def _():
+        down.wait_send()
+        up.wait_recv()
+
+    @pl.when(place == 0)
+    def _():
+        below[...] = jnp.zeros_like(below)
+
+    lax.fori_loop(0, 2, lower, 0)
+    lax.fori_loop(0, 2, upper, 0)
 
     def first(plane, carry):
         inside = jnp.logical_and(
@@ -302,7 +416,48 @@
         return carry
 
     lax.fori_loop(0, cells_x + 2, first, 0)
-    build_weights(1)
+
+    finish(copies)
+    modes[...] = lax.dot_general(
+        lands[1], y_in_ref[...], (((0,), (1,)), ((), ())),
+        precision=HIGHEST, preferred_element_type=jnp.float32,
+    )
+    weight_copy.wait()
+    group = 4
+
+    def mix_rows(step, carry):
+        q = step % (MZ // 4)
+        g = step // (MZ // 4)
+        lines = pl.ds(pl.multiple_of(q * 128, 128), 128)
+        width = group * owned_x * 2
+        cols = pltpu.roll(modes[lines, :], lax.rem(modes.shape[1] - g * width, modes.shape[1]), 1)
+        for y in range(group):
+            for x in range(owned_x):
+                spot = (y * owned_x + x) * 2
+                reals, imags = [], []
+                for k in range(4):
+                    real = jnp.broadcast_to(cols[k * CH : (k + 1) * CH, spot : spot + 1], (CH, CH))
+                    imag = jnp.broadcast_to(cols[k * CH : (k + 1) * CH, spot + 1 : spot + 2], (CH, CH))
+                    weight_real = weights[g * group + y, x, q * 4 + k, 0]
+                    weight_imag = weights[g * group + y, x, q * 4 + k, 1]
+                    out_real = real * weight_real - imag * weight_imag
+                    out_imag = real * weight_imag + imag * weight_real
+                    reals.append(out_real.reshape(CH // 8, 8, CH).sum(0))
+                    imags.append(out_imag.reshape(CH // 8, 8, CH).sum(0))
+                for ri, parts in enumerate((reals, imags)):
+                    mixed[q, pl.ds(g * width + spot + ri, 1), :] = jnp.sum(
+                        jnp.concatenate(parts, axis=1), axis=0, keepdims=True
+                    )
+        return carry
+
+    lax.fori_loop(0, (MZ // 4) * (MY // group), mix_rows, 0)
+    for q in range(MZ // 4):
+        sends[2, :, q * 128 : (q + 1) * 128] = jnp.dot(
+            y_out_ref[...], mixed[q], precision=HIGHEST, preferred_element_type=jnp.float32
+        )
+    copies = exchange(2)
+
+    build_weights(second_ref)
 
     def rebuild(plane, carry):
         def fetch(column, width):
@@ -315,29 +470,88 @@
 
     lax.fori_loop(0, cells_x + 2, rebuild, 0)
 
+    finish(copies)
+    sends[3] = jnp.dot(x_out_ref[...], lands[2], precision=HIGHEST, preferred_element_type=jnp.float32)
+    copies = exchange(3)
+
     def second(plane, carry):
         total = multiply(plane)
         for b in range(BLOCKS):
-            out_ref[plane, :, b * LANES : (b + 1) * LANES] = total[b * cells_y : (b + 1) * cells_y]
+            out_ref[plane, :, b * LANES : (b + 1) * LANES] = (
+                total[b * cells_y : (b + 1) * cells_y] + bias_ref[...]
+            )
         return carry
 
     lax.fori_loop(0, cells_x, second, 0)
 
-
-def two_convolutions(field, conv_first, conv_second):
+    finish(copies)
+    for q in range(mode_width // 128):
+        spectrum[q] = lands[3, :, q * 128 : (q + 1) * 128]
+    lines = []
+    for x in range(cells_x):
+        lines.append(
+            jnp.concatenate(
+                [
+                    spectrum[q, pl.ds(x * 2 + ri, cells_y, stride=2 * cells_x), :]
+                    for ri in range(2)
+                    for q in range(mode_width // 128)
+                ],
+                axis=1,
+            )
+        )
+    line_high, line_low = split_bf16(jnp.concatenate(lines, axis=0) * scale_ref[...])
+    across = (((1,), (1,)), ((), ()))
+    for b in range(BLOCKS):
+        rows = slice(b * LANES, (b + 1) * LANES)
+        part = lax.dot_general(line_high, z_high[rows, :], across, preferred_element_type=jnp.float32)
+        part += lax.dot_general(line_high, z_low[rows, :], across, preferred_element_type=jnp.float32)
+        part += lax.dot_general(line_low, z_high[rows, :], across, preferred_element_type=jnp.float32)
+        for x in range(cells_x):
+            out_ref[x, :, rows] = gelu(out_ref[x, :, rows] + part[x * cells_y : (x + 1) * cells_y])
+
+
+def kept_list(length, retained):
+    spots = np.arange(retained)
+    return np.where(spots < retained // 2, spots, length - retained + spots)
+
+
+def rotation(angle_index, length, inverse):
+    angle = angle_index % length * (2.0 * math.pi / length)
+    cos, sin = np.cos(angle), np.sin(angle)
+    sign = -1.0 if inverse else 1.0
+    return np.stack([np.stack([cos, sign * sin], -1), np.stack([-sign * sin, cos], -1)], -2)
+
+
+def tables(cells_x, cells_y, count):
+    extent_x, owned_x, rows_y = cells_x * count, MX // count, cells_y // count
+    x_turn = rotation(kept_list(extent_x, MX)[:, None] * np.arange(extent_x)[None], extent_x, False)
+    y_turn = rotation(kept_list(cells_y, MY)[:, None] * np.arange(cells_y)[None], cells_y, False)
+    x_turn = x_turn.reshape(count, owned_x, count, cells_x, 2, 2)
+    y_turn = y_turn.reshape(MY, count, rows_y, 2, 2)
+    same_y, same_x = np.eye(rows_y), np.eye(owned_x)
+    x_in = np.einsum("ekdxab,yw->ekyadwxb", x_turn, same_y).reshape(count * owned_x * rows_y * 2, -1)
+    y_in = np.einsum("ldyab,kj->lkadjyb", y_turn, same_x).reshape(MY * owned_x * 2, -1)
+    y_out = np.einsum("leyba,kj->eykaljb", y_turn, same_x).reshape(count * rows_y * owned_x * 2, -1)
+    x_out = np.einsum("dkexba,yw->eyxadwkb", x_turn, same_y).reshape(count * rows_y * cells_x * 2, -1)
+    angle = np.arange(NZ)[:, None] * np.arange(MZ)[None] % NZ * (2.0 * math.pi / NZ)
+    z_table = np.repeat(np.stack([np.cos(angle), -np.sin(angle)], 1).reshape(NZ, 2 * MZ), CH, axis=1)
+    scale = np.where(np.arange(MZ) == 0, 1.0, 2.0) / (extent_x * cells_y * NZ)
+    scale = np.repeat(np.tile(scale, 2), CH)[None]
+    return [jnp.asarray(t, jnp.float32) for t in (z_table, scale, x_in, y_in, y_out, x_out)]
+
+
+def line_body(field, spectral, conv_first, conv_second, bias):
     cells_x, cells_y, merged_width = field.shape
     count = lax.axis_size("gx")
-    pairs = [(i, i + 1) for i in range(count - 1)]
-    below = lax.ppermute(field[cells_x - 2 :], "gx", pairs)
-    above = lax.ppermute(field[:2], "gx", [(j, i) for i, j in pairs])
-    tiled = jnp.tile(jnp.stack([conv_first, conv_second]).reshape(2, 27, CH, CH), (1, 1, 1, STEP))
+    mode_width = MZ * CH
+    total_rows = cells_x * cells_y * 2
     rows = BLOCKS * cells_y
     vmem = pl.BlockSpec(memory_space=pltpu.VMEM)
-    flops = 2 * 3 * 3 * (2 * cells_x + 2) * rows * DEPTH * LANES
+    quarter = mode_width // 128
     return pl.pallas_call(
-        conv_kernel,
+        functools.partial(block_kernel, count),
         out_shape=jax.ShapeDtypeStruct(field.shape, jnp.float32),
-        in_specs=[vmem] * 4,
+        in_specs=[vmem, pl.BlockSpec(memory_space=pl.ANY)] + [vmem] * 9,
         out_specs=vmem,
         scratch_shapes=[
             pltpu.VMEM((3, DEPTH, LANES), jnp.bfloat16),
@@ -345,91 +559,29 @@
             pltpu.VMEM((cells_x + 4, rows, DEPTH), jnp.bfloat16),
             pltpu.VMEM((cells_x + 4, rows, DEPTH), jnp.bfloat16),
             pltpu.VMEM((cells_x + 2, rows, LANES), jnp.float32),
+            pltpu.VMEM((merged_width, 2 * mode_width), jnp.bfloat16),
+            pltpu.VMEM((merged_width, 2 * mode_width), jnp.bfloat16),
+            pltpu.VMEM(spectral.shape, jnp.float32),
+            pltpu.VMEM((mode_width, total_rows), jnp.float32),
+            pltpu.VMEM((quarter, total_rows, 128), jnp.float32),
+            pltpu.VMEM((quarter, total_rows, 128), jnp.float32),
+            pltpu.VMEM((2, cells_y, merged_width), jnp.float32),
+            pltpu.VMEM((2, cells_y, merged_width), jnp.float32),
+            pltpu.VMEM((4, total_rows, mode_width), jnp.float32),
+            pltpu.VMEM((4, total_rows, mode_width), jnp.float32),
+            pltpu.SemaphoreType.DMA((4, count)),
+            pltpu.SemaphoreType.DMA((4, count)),
+            pltpu.SemaphoreType.DMA((2,)),
+            pltpu.SemaphoreType.DMA((2,)),
+            pltpu.SemaphoreType.DMA,
         ],
-        cost_estimate=pl.CostEstimate(flops=flops, bytes_accessed=8 * field.size, transcendentals=0),
-        compiler_params=pltpu.CompilerParams(vmem_limit_bytes=28 * 2**20),
-    )(field, below, above, tiled)
-
-
-def mix_kernel(modes_ref, weight_ref, out_ref):
-    rows, owned_x, depth = weight_ref.shape[:3]
-    mode = 0
-    for y in range(rows):
-        for x in range(owned_x):
-            for k in range(depth):
-                real = jnp.broadcast_to(modes_ref[0, 0, :, mode : mode + 1], (CH, CH))
-                imag = jnp.broadcast_to(modes_ref[0, 1, :, mode : mode + 1], (CH, CH))
-                weight_real = weight_ref[y, x, k, 0]
-                weight_imag = weight_ref[y, x, k, 1]
-                out_ref[0, 0, mode : mode + 1, :] = jnp.sum(
-                    real * weight_real - imag * weight_imag, axis=0, keepdims=True
-                )
-                out_ref[0, 1, mode : mode + 1, :] = jnp.sum(
-                    real * weight_imag + imag * weight_real, axis=0, keepdims=True
-                )
-                mode += 1
-
-
-def mix_modes(complex_parts, spectral):
-    rows, owned_x = spectral.shape[:2]
-    per = 2
-    count = per * owned_x * MZ
-    steps = rows // per
-    modes = complex_parts.reshape(steps, per, owned_x, 2, MZ, CH).transpose(0, 3, 5, 1, 2, 4)
-    out = pl.pallas_call(
-        mix_kernel,
-        grid=(steps,),
-        out_shape=jax.ShapeDtypeStruct((steps, 2, count, CH), jnp.float32),
-        in_specs=[
-            pl.BlockSpec((1, 2, CH, count), lambda i: (i, 0, 0, 0)),
-            pl.BlockSpec((per, owned_x, MZ, 2, CH, CH), lambda i: (i, 0, 0, 0, 0, 0)),
-        ],
-        out_specs=pl.BlockSpec((1, 2, count, CH), lambda i: (i, 0, 0, 0)),
-        cost_estimate=pl.CostEstimate(flops=8 * spectral.size, bytes_accessed=16 * spectral.size, transcendentals=0),
-    )(modes.reshape(steps, 2, CH, count), spectral)
-    return out.reshape(steps, 2, per, owned_x, MZ, CH).transpose(0, 2, 3, 1, 4, 5)
-
-
-def complex_table(cos_table, sin_table, sign):
-    top = jnp.stack([cos_table, sign * sin_table], axis=1)
-    bottom = jnp.stack([-sign * sin_table, cos_table], axis=1)
-    return jnp.stack([top, bottom], axis=0)
-
-
-def line_body(field, spectral, conv_first, conv_second, bias):
-    cells_x, cells_y, merged_width = field.shape
-    devices_x = lax.axis_size("gx")
-    extent_x = cells_x * devices_x
-    extent_y = cells_y
-    owned_x = MX // devices_x
-    mode_width = MZ * CH
-    second_branch = two_convolutions(field, conv_first, conv_second)
-    z_index = jnp.arange(MZ, dtype=jnp.int32)
-    z_cos, z_sin = angle_table(z_index, jnp.arange(NZ, dtype=jnp.int32), NZ)
-    volume = field.reshape(cells_x, cells_y, NZ, CH)
-    forward_z = jnp.stack([z_cos, -z_sin])
-    z_spectrum = jnp.einsum("xyzc,rkz->xyrkc", volume, forward_z, precision=HIGH)
-    z_spectrum = z_spectrum.reshape(cells_x, cells_y, 2, mode_width)
-    kept_x = frequency(jnp.arange(MX, dtype=jnp.int32), extent_x, MX)
-    kept_y = frequency(jnp.arange(MY, dtype=jnp.int32), extent_y, MY)
-    x_table = complex_table(*angle_table(kept_x, jnp.arange(extent_x, dtype=jnp.int32), extent_x), 1.0)
-    y_table = complex_table(*angle_table(kept_y, jnp.arange(extent_y, dtype=jnp.int32), extent_y), 1.0)
-    lines = lax.all_to_all(z_spectrum, "gx", split_axis=1, concat_axis=0, tiled=True)
-    kept = jnp.einsum("akbx,xybm->kyam", x_table, lines, precision=HIGH)
-    x_modes = lax.all_to_all(kept, "gx", split_axis=0, concat_axis=1, tiled=True)
-    all_modes = jnp.einsum("akby,xybm->kxam", y_table, x_modes, precision=HIGH)
-    mixed = mix_modes(all_modes, spectral).reshape(MY, owned_x, 2, mode_width)
-    y_cells = jnp.einsum("bkay,kxbm->xyam", y_table, mixed, precision=HIGH)
-    lines = lax.all_to_all(y_cells, "gx", split_axis=1, concat_axis=0, tiled=True)
-    lines = jnp.einsum("bkax,kybm->xyam", x_table, lines, precision=HIGH)
-    planes = lax.all_to_all(lines, "gx", split_axis=0, concat_axis=1, tiled=True)
-    weights = jnp.where(z_index == 0, 1.0, 2.0).astype(jnp.float32) / (extent_x * extent_y * NZ)
-    back_z = jnp.stack([z_cos * weights[:, None], -z_sin * weights[:, None]])
-    spectral_part = jnp.einsum(
-        "xyrkc,rkz->xyzc", planes.reshape(cells_x, cells_y, 2, MZ, CH), back_z, precision=HIGH
-    )
-    total = spectral_part.reshape(field.shape) + second_branch + jnp.tile(bias, NZ)
-    return jax.nn.gelu(total, approximate=False)
+        compiler_params=pltpu.CompilerParams(
+            collective_id=0, has_side_effects=True, vmem_limit_bytes=63 * 2**20
+        ),
+    )(
+        field, spectral, conv_first.reshape(27, CH, CH), conv_second.reshape(27, CH, CH),
+        jnp.tile(bias, STEP)[None], *tables(cells_x, cells_y, count),
+    )
 
 
 def solution(mesh):
@@ -441,5 +593,11 @@
         P(),
     )
     out_specs = P(("groups", "gx"), "gy", None)
-    chosen = line_body if mesh.shape["gy"] == 1 else body
+    count = mesh.shape["gx"]
+
+    def chosen(field, *rest):
+        whole = (field.shape[0] * count, field.shape[1] * mesh.shape["gy"])
+        fits = whole == (MX, MY) and mesh.shape["gy"] == 1 and MX == MY == 2 * count
+        return (line_body if fits else body)(field, *rest)
+
     return jax.shard_map(chosen, mesh=mesh, in_specs=in_specs, out_specs=out_specs, check_vma=False)

time: 116 us -> 86.4 us (0.74)
  Pallas kernels: 33.7 us -> 83.1 us
  local copies, waits for them, and re-layouts: 28.9 us -> 3.17 us
  starting transfers between devices: 23.1 us -> 0 us
  blocking collectives: 12.7 us -> 0 us
  waiting for transfers between devices: 9.83 us -> 0 us
  matrix products: 3.83 us -> 0 us
  other arithmetic: 2.33 us -> 0 us
    pallas_call x2 -> x1, Pallas kernels: 33.7 us -> 83.1 us  [line_body(): pl.pallas_call(functools.partial(block_kernel, count), out_shape=jax.Shap...]
    all_to_all x3 -> x0, starting transfers between devices: 19.7 us -> none  [the longest x1 8.09 us: line_body(): lax.all_to_all(lines, 'gx', split_axis=0, concat_axis=1, tiled=True)]
    all_to_all x1 -> x0, blocking collectives: 12.7 us -> none  [line_body(): lax.all_to_all(kept, 'gx', split_axis=0, concat_axis=1, tiled=True)]
    all_to_all x3 -> x0, waiting for transfers between devices: 9.83 us -> none  [the longest x1 9.82 us: line_body(): lax.all_to_all(z_spectrum, 'gx', split_axis=1, concat_axis=0, tiled=True)]
    reshape x9 -> x0, local copies, waits for them, and re-layouts: 8.02 us -> none  [the longest x1 2.5 us: line_body(): spectral_part.reshape(field.shape) + second_branch + jnp.tile(bias, NZ)]
    another operation x3 -> x2, local copies, waits for them, and re-layouts: 8.47 us -> 1.3 us  [line_body(): jnp.tile(bias, STEP)[None]]
    transpose x5 -> x0, local copies, waits for them, and re-layouts: 5.44 us -> none  [the longest x1 1.97 us: line_body(): jnp.einsum('xyrkc,rkz->xyzc', planes.reshape(cells_x, cells_y, 2, MZ, CH)...]
    all_to_all x7 -> x0, local copies, waits for them, and re-layouts: 5.09 us -> none  [the longest x2 3.61 us: line_body(): lax.all_to_all(y_cells, 'gx', split_axis=1, concat_axis=0, tiled=True)]
  transfers between devices with their start and end apart: 5 -> 0, of which waited for: 1 -> 0; matrix products, arithmetic and copies ran while one was open for 13% -> 0% of each run, Pallas kernels for 11% -> 0%
where the time goes in v2:
time: 86.4 us; the launch traced here: 86.2 us
  Pallas kernels  83.1 us (96%)
  local copies, waits for them, and re-layouts  3.17 us (4%)
    pallas_call x1, Pallas kernels, line_body(): pl.pallas_call(functools.partial(block_kernel, count), out_shape=jax.Shap...  83.1 us
    unnamed x1, local copies, waits for them, and re-layouts  1.87 us

profile of v2, /device:TPU:0, one launch (start us, length us, event | category | flops | bytes accessed | tf_op | source)
XLA Modules:
  0.0 86.2 jit_solution(2412998651514571572)
XLA Ops:
  0.0 0.7 tile.2
  0.7 0.6 broadcast_in_dim_tile.3.bias_ref
  1.3 83.1 %shard_map.109 = f32[2,32,2048]{2,1,0:T(8,128)} custom-call(f32[2,32,2048]{2,1,0:T(8,128)} %body_ref.1, f32[32,2,16,2,32,32]{5,4,3,2,1,0:T(8,128)} %spectral_ref.1, f32[27,32,32]{2,1,0:T(8,128)} %bitcast.2, f32[27,32,32]{2,1,0:T(8,128)} %bitcast.3, f32[1,256]{1,0:T(1,128)} %broadcast_in_dim_tile.3.bias_ref, f32[64,1024]{1,0:T(8,128)} %constant.10.clone.z_ref, ...), custom_call_target="tpu_custom_call" | custom-call | tf_op jit(solution)/shard_map/pallas_call | solution.py:551
  84.4 1.9 %copy.13 = f32[2,32,2048]{2,1,0:T(8,128)} copy(f32[2,32,2048]{2,1,0:T(8,128)} %shard_map.109) | data formatting | bytes 1048576

commit v3 on v2

--- a/solution.py
+++ b/solution.py
@@ -202,7 +202,7 @@
 def block_kernel(
     count, body_ref, spectral_ref, first_ref, second_ref, bias_ref, z_ref, scale_ref,
     x_in_ref, y_in_ref, y_out_ref, x_out_ref, out_ref,
-    b_high, b_low, a_high, a_low, hidden, z_high, z_low, weights, modes, mixed, spectrum,
+    b_high, b_low, a_high, a_low, hidden, z_high, z_low, slots, packed, spectrum,
     below, above, sends, lands, send_sems, land_sems, halo_send, halo_land, weight_sem,
 ):
     cells_x, cells_y, merged_width = body_ref.shape
@@ -217,8 +217,36 @@
         pl.semaphore_signal(
             barrier, inc=1, device_id={"gx": lax.rem(place + offset, count)}, device_id_type=MESH
         )
-    weight_copy = pltpu.make_async_copy(spectral_ref, weights, weight_sem)
-    weight_copy.start()
+    slot_count, per_slot = slots.shape[:2]
+    chunks = MY // per_slot
+    pairs = MY * owned_x
+    quarter = mode_width // 128
+
+    def weight_copy(chunk):
+        slot = lax.rem(chunk, slot_count)
+        return pltpu.make_async_copy(
+            spectral_ref.at[pl.ds(chunk * per_slot, per_slot)], slots.at[slot], weight_sem.at[slot]
+        )
+
+    for chunk in range(slot_count):
+        weight_copy(chunk).start()
+
+    def pack(chunk, carry):
+        weight_copy(chunk).wait()
+        slot = lax.rem(chunk, slot_count)
+        for y in range(per_slot):
+            for x in range(owned_x):
+                pair = (chunk * per_slot + y) * owned_x + x
+                for q in range(quarter):
+                    for ri in range(2):
+                        tile = jnp.concatenate([slots[slot, y, x, q * 4 + k, ri] for k in range(4)], axis=0)
+                        packed[q, ri, pl.ds(pair, CH, stride=pairs), :] = tile.T
+
+        @pl.when(chunk + slot_count < chunks)
+        def _():
+            weight_copy(chunk + slot_count).start()
+
+        return carry
 
     def at(index):
         return pl.ds(pl.multiple_of(index * block, 8), block)
@@ -281,14 +309,6 @@
         src_ref=body_ref.at[pl.ds(0, 2)], dst_ref=above, send_sem=halo_send.at[1],
         recv_sem=halo_land.at[1], device_id={"gx": lax.rem(place + last, count)}, device_id_type=MESH,
     )
-
-    @pl.when(place < last)
-    def _():
-        up.start()
-
-    @pl.when(place > 0)
-    def _():
-        down.start()
 
     lane_block = lax.broadcasted_iota(jnp.int32, (CH, LANES), 1) // CH
 
@@ -379,12 +399,61 @@
         build_plane(cells_x + 2 + x, from_ref(above, x))
         return carry
 
-    build_weights(first_ref)
-    lax.fori_loop(0, cells_x, inner, 0)
+    lax.fori_loop(0, chunks // 2, pack, 0)
 
     finish(copies)
     sends[1] = jnp.dot(x_in_ref[...], lands[0], precision=HIGHEST, preferred_element_type=jnp.float32)
     copies = exchange(1)
+
+    lax.fori_loop(chunks // 2, chunks, pack, 0)
+
+    finish(copies)
+    @pl.when(place < last)
+    def _():
+        up.start()
+
+    @pl.when(place > 0)
+    def _():
+        down.start()
+
+    modes = jnp.dot(y_in_ref[...], lands[1], precision=HIGHEST, preferred_element_type=jnp.float32)
+    for q in range(quarter):
+        spectrum[q] = modes[:, q * 128 : (q + 1) * 128]
+    height = 2 * pairs
+
+    def mix(step, total):
+        rows = []
+        for q in range(quarter):
+            real, imag = spectrum[q, :pairs], spectrum[q, pairs:]
+            columns = []
+            for half in range(2):
+                lines = pl.ds(pl.multiple_of((2 * step + half) * pairs, pairs), pairs)
+                weight_real, weight_imag = packed[q, 0, lines, :], packed[q, 1, lines, :]
+                columns.append(
+                    jnp.concatenate(
+                        [real * weight_real - imag * weight_imag, real * weight_imag + imag * weight_real],
+                        axis=0,
+                    )
+                )
+            rows.append(jnp.concatenate(columns, axis=1))
+        high, low = split_bf16(jnp.concatenate(rows, axis=0))
+        source = lax.broadcasted_iota(jnp.int32, (256, 128), 0)
+        target = lax.broadcasted_iota(jnp.int32, (256, 128), 1)
+        place_of = (source % 128) // CH * CH + 2 * step + source // 128
+        gather = jnp.where(place_of == target, 1.0, 0.0).astype(jnp.bfloat16)
+        total += jnp.dot(high, gather, preferred_element_type=jnp.float32)
+        return total + jnp.dot(low, gather, preferred_element_type=jnp.float32)
+
+    mixed = lax.fori_loop(0, CH // 2, mix, jnp.zeros((quarter * height, 128), jnp.float32))
+    for q in range(quarter):
+        sends[2, :, q * 128 : (q + 1) * 128] = jnp.dot(
+            y_out_ref[...], mixed[q * height : (q + 1) * height],
+            precision=HIGHEST, preferred_element_type=jnp.float32,
+        )
+    copies = exchange(2)
+
+    build_weights(first_ref)
+    lax.fori_loop(0, cells_x, inner, 0)
 
     @pl.when(place < last)
     def _():
@@ -418,44 +487,8 @@
     lax.fori_loop(0, cells_x + 2, first, 0)
 
     finish(copies)
-    modes[...] = lax.dot_general(
-        lands[1], y_in_ref[...], (((0,), (1,)), ((), ())),
-        precision=HIGHEST, preferred_element_type=jnp.float32,
-    )
-    weight_copy.wait()
-    group = 4
-
-    def mix_rows(step, carry):
-        q = step % (MZ // 4)
-        g = step // (MZ // 4)
-        lines = pl.ds(pl.multiple_of(q * 128, 128), 128)
-        width = group * owned_x * 2
-        cols = pltpu.roll(modes[lines, :], lax.rem(modes.shape[1] - g * width, modes.shape[1]), 1)
-        for y in range(group):
-            for x in range(owned_x):
-                spot = (y * owned_x + x) * 2
-                reals, imags = [], []
-                for k in range(4):
-                    real = jnp.broadcast_to(cols[k * CH : (k + 1) * CH, spot : spot + 1], (CH, CH))
-                    imag = jnp.broadcast_to(cols[k * CH : (k + 1) * CH, spot + 1 : spot + 2], (CH, CH))
-                    weight_real = weights[g * group + y, x, q * 4 + k, 0]
-                    weight_imag = weights[g * group + y, x, q * 4 + k, 1]
-                    out_real = real * weight_real - imag * weight_imag
-                    out_imag = real * weight_imag + imag * weight_real
-                    reals.append(out_real.reshape(CH // 8, 8, CH).sum(0))
-                    imags.append(out_imag.reshape(CH // 8, 8, CH).sum(0))
-                for ri, parts in enumerate((reals, imags)):
-                    mixed[q, pl.ds(g * width + spot + ri, 1), :] = jnp.sum(
-                        jnp.concatenate(parts, axis=1), axis=0, keepdims=True
-                    )
-        return carry
-
-    lax.fori_loop(0, (MZ // 4) * (MY // group), mix_rows, 0)
-    for q in range(MZ // 4):
-        sends[2, :, q * 128 : (q + 1) * 128] = jnp.dot(
-            y_out_ref[...], mixed[q], precision=HIGHEST, preferred_element_type=jnp.float32
-        )
-    copies = exchange(2)
+    sends[3] = jnp.dot(x_out_ref[...], lands[2], precision=HIGHEST, preferred_element_type=jnp.float32)
+    copies = exchange(3)
 
     build_weights(second_ref)
 
@@ -469,10 +502,6 @@
         return carry
 
     lax.fori_loop(0, cells_x + 2, rebuild, 0)
-
-    finish(copies)
-    sends[3] = jnp.dot(x_out_ref[...], lands[2], precision=HIGHEST, preferred_element_type=jnp.float32)
-    copies = exchange(3)
 
     def second(plane, carry):
         total = multiply(plane)
@@ -530,8 +559,8 @@
     y_turn = y_turn.reshape(MY, count, rows_y, 2, 2)
     same_y, same_x = np.eye(rows_y), np.eye(owned_x)
     x_in = np.einsum("ekdxab,yw->ekyadwxb", x_turn, same_y).reshape(count * owned_x * rows_y * 2, -1)
-    y_in = np.einsum("ldyab,kj->lkadjyb", y_turn, same_x).reshape(MY * owned_x * 2, -1)
-    y_out = np.einsum("leyba,kj->eykaljb", y_turn, same_x).reshape(count * rows_y * owned_x * 2, -1)
+    y_in = np.einsum("ldyab,kj->alkdjyb", y_turn, same_x).reshape(MY * owned_x * 2, -1)
+    y_out = np.einsum("leyba,kj->eykablj", y_turn, same_x).reshape(count * rows_y * owned_x * 2, -1)
     x_out = np.einsum("dkexba,yw->eyxadwkb", x_turn, same_y).reshape(count * rows_y * cells_x * 2, -1)
     angle = np.arange(NZ)[:, None] * np.arange(MZ)[None] % NZ * (2.0 * math.pi / NZ)
     z_table = np.repeat(np.stack([np.cos(angle), -np.sin(angle)], 1).reshape(NZ, 2 * MZ), CH, axis=1)
@@ -561,9 +590,8 @@
             pltpu.VMEM((cells_x + 2, rows, LANES), jnp.float32),
             pltpu.VMEM((merged_width, 2 * mode_width), jnp.bfloat16),
             pltpu.VMEM((merged_width, 2 * mode_width), jnp.bfloat16),
-            pltpu.VMEM(spectral.shape, jnp.float32),
-            pltpu.VMEM((mode_width, total_rows), jnp.float32),
-            pltpu.VMEM((quarter, total_rows, 128), jnp.float32),
+            pltpu.VMEM((4, 2) + spectral.shape[1:], jnp.float32),
+            pltpu.VMEM((quarter, 2, CH * MY * spectral.shape[1], 128), jnp.float32),
             pltpu.VMEM((quarter, total_rows, 128), jnp.float32),
             pltpu.VMEM((2, cells_y, merged_width), jnp.float32),
             pltpu.VMEM((2, cells_y, merged_width), jnp.float32),
@@ -573,7 +601,7 @@
             pltpu.SemaphoreType.DMA((4, count)),
             pltpu.SemaphoreType.DMA((2,)),
             pltpu.SemaphoreType.DMA((2,)),
-            pltpu.SemaphoreType.DMA,
+            pltpu.SemaphoreType.DMA((4,)),
         ],
         compiler_params=pltpu.CompilerParams(
             collective_id=0, has_side_effects=True, vmem_limit_bytes=63 * 2**20

time: 86.4 us -> 62.3 us (0.72)
  Pallas kernels: 83.1 us -> 59 us
    pallas_call x1, Pallas kernels: 83.1 us -> 59 us  [line_body(): pl.pallas_call(functools.partial(block_kernel, count), out_shape=jax.Shap...]
where the time goes in v3:
time: 62.3 us; the launch traced here: 62.1 us
  Pallas kernels  59 us (95%)
  local copies, waits for them, and re-layouts  3.17 us (5%)
    pallas_call x1, Pallas kernels, line_body(): pl.pallas_call(functools.partial(block_kernel, count), out_shape=jax.Shap...  59 us
    unnamed x1, local copies, waits for them, and re-layouts  1.87 us
    another operation x2, local copies, waits for them, and re-layouts, line_body(): jnp.tile(bias, STEP)[None]  1.3 us

profile of v3, /device:TPU:0, one launch (start us, length us, event | category | flops | bytes accessed | tf_op | source)
XLA Modules:
  0.0 62.1 jit_solution(13749326233637300415)
XLA Ops:
  0.0 0.7 %tile.2 = f32[8,32]{1,0:T(8,128)S(1)} broadcast(f32[32]{0:T(128)} %param.15), dimensions={1} | broadcast | bytes 1152 | tf_op jit(solution)/shard_map/tile | solution.py:611
  0.7 0.6 %broadcast_in_dim_tile.3.bias_ref = f32[1,256]{1,0:T(1,128)} reshape(f32[8,32]{1,0:T(8,128)S(1)} %tile.2) | data formatting | bytes 2048 | tf_op jit(solution)/shard_map/broadcast_in_dim;tile | solution.py:611
  1.3 59.0 %shard_map.109 = f32[2,32,2048]{2,1,0:T(8,128)} custom-call(f32[2,32,2048]{2,1,0:T(8,128)} %body_ref.1, f32[32,2,16,2,32,32]{5,4,3,2,1,0:T(8,128)} %spectral_ref.1, f32[27,32,32]{2,1,0:T(8,128)} %bitcast.2, f32[27,32,32]{2,1,0:T(8,128)} %bitcast.3, f32[1,256]{1,0:T(1,128)} %broadcast_in_dim_tile.3.bias_ref, f32[64,1024]{1,0:T(8,128)} %constant.12.clone.z_ref, ...), custom_call_target="tpu_custom_call" | custom-call | tf_op jit(solution)/shard_map/pallas_call | solution.py:580
  60.3 1.9 %copy.13 = f32[2,32,2048]{2,1,0:T(8,128)} copy(f32[2,32,2048]{2,1,0:T(8,128)} %shard_map.109) | data formatting | bytes 1048576

commit v4 on v3

--- a/solution.py
+++ b/solution.py
@@ -400,12 +400,14 @@
         return carry
 
     lax.fori_loop(0, chunks // 2, pack, 0)
+    build_weights(first_ref)
 
     finish(copies)
     sends[1] = jnp.dot(x_in_ref[...], lands[0], precision=HIGHEST, preferred_element_type=jnp.float32)
     copies = exchange(1)
 
     lax.fori_loop(chunks // 2, chunks, pack, 0)
+    lax.fori_loop(0, cells_x, inner, 0)
 
     finish(copies)
     @pl.when(place < last)
@@ -452,8 +454,6 @@
         )
     copies = exchange(2)
 
-    build_weights(first_ref)
-    lax.fori_loop(0, cells_x, inner, 0)
 
     @pl.when(place < last)
     def _():
@@ -503,11 +503,13 @@
 
     lax.fori_loop(0, cells_x + 2, rebuild, 0)
 
+    shift = jnp.concatenate([bias_ref[...]] * STEP, axis=1)
+
     def second(plane, carry):
         total = multiply(plane)
         for b in range(BLOCKS):
             out_ref[plane, :, b * LANES : (b + 1) * LANES] = (
-                total[b * cells_y : (b + 1) * cells_y] + bias_ref[...]
+                total[b * cells_y : (b + 1) * cells_y] + shift
             )
         return carry
 
@@ -608,7 +610,7 @@
         ),
     )(
         field, spectral, conv_first.reshape(27, CH, CH), conv_second.reshape(27, CH, CH),
-        jnp.tile(bias, STEP)[None], *tables(cells_x, cells_y, count),
+        bias[None], *tables(cells_x, cells_y, count),
     )
 
 

time: 62.3 us -> 62 us (level)
  local copies, waits for them, and re-layouts: 3.17 us -> 1.87 us
  Pallas kernels: 59 us -> 59.9 us
    another operation x2 -> x0, local copies, waits for them, and re-layouts: 1.3 us -> none  [line_body(): jnp.tile(bias, STEP)[None]]
    pallas_call x1, Pallas kernels: 59 us -> 59.9 us  [line_body(): pl.pallas_call(functools.partial(block_kernel, count), out_shape=jax.Shap...]
where the time goes in v4:
time: 62 us; the launch traced here: 61.8 us
  Pallas kernels  59.9 us (97%)
  local copies, waits for them, and re-layouts  1.87 us (3%)
    pallas_call x1, Pallas kernels, line_body(): pl.pallas_call(functools.partial(block_kernel, count), out_shape=jax.Shap...  59.9 us
    unnamed x1, local copies, waits for them, and re-layouts  1.87 us

profile of v4, /device:TPU:0, one launch (start us, length us, event | category | flops | bytes accessed | tf_op | source)
XLA Modules:
  0.0 61.8 jit_solution(5171035775206917106)
XLA Ops:
  0.0 59.9 %shard_map.109 = f32[2,32,2048]{2,1,0:T(8,128)} custom-call(f32[2,32,2048]{2,1,0:T(8,128)} %body_ref.1, f32[32,2,16,2,32,32]{5,4,3,2,1,0:T(8,128)} %spectral_ref.1, f32[27,32,32]{2,1,0:T(8,128)} %bitcast.3, f32[27,32,32]{2,1,0:T(8,128)} %bitcast.4, f32[1,32]{1,0:T(1,128)} %bitcast.5, f32[64,1024]{1,0:T(8,128)} %constant.12.clone.z_ref, ...), custom_call_target="tpu_custom_call" | custom-call | tf_op jit(solution)/shard_map/pallas_call | solution.py:582
  59.9 1.9 %copy.13 = f32[2,32,2048]{2,1,0:T(8,128)} copy(f32[2,32,2048]{2,1,0:T(8,128)} %shard_map.109) | data formatting | bytes 1048576
